TPU v7x, 256 devices: a whole 4x4x8 slice. The times are simulated.
256 devices in a mesh: dp: 8 (over y, z_lo), space: 32 (over x, z_hi, core).
Axes of the slice: x: 4, y: 4, z: 8 (z_hi: 4, z_lo: 2; z = z_hi * 2 + z_lo), core: 2. Of those that a mesh axis runs over, the one named last changes fastest.
Arguments:
- inputs: bfloat16 [8, 32, 48, 4096], P('dp', 'space'), may hold values from -6 to 6
- cotangent: bfloat16 [8, 32, 48, 4096], P('dp', 'space'), may hold values from -6 to 6
- conv_one: bfloat16 [9, 48, 48], replicated, may hold values from -0.3125 to 0.3125
- bias_one: float32 [48], replicated, may hold values from -3 to 3
- conv_two: bfloat16 [9, 48, 48], replicated, may hold values from -0.3125 to 0.3125
- bias_two: float32 [48], replicated, may hold values from -3 to 3
- neighbours: int32 [32, 4, 3], replicated, may hold values from 0 to 31, as said below
- corner_rule: int32 [32, 4], replicated, may hold values from 0 to 2
Outputs:
- output: bfloat16 [8, 32, 48, 4096], P('dp', 'space')
- grad_in: bfloat16 [8, 32, 48, 4096], P('dp', 'space')
- grad_conv_one: float32 [9, 48, 48], P(None, 'dp')
- grad_bias_one: float32 [48], P('dp')
- grad_conv_two: float32 [9, 48, 48], P(None, 'dp')
- grad_bias_two: float32 [48], P('dp')
Inputs may be any that keep to these rules, and one draw needn't show every extreme that they name: Slot neighbours[t, e, 0] of a tile on the device block d (tiles d * 1 to d + 1 - 1) lies on block d - 1, d + 8, d + 1, d - 8 (cyclically over the 32 blocks) for e = 0, 1, 2, 3; neighbours[t, e, 1] and neighbours[t, e, 2] are 0 to 3.
All inputs are finite; a program needn't handle non-finite values.
Results may differ from a plain program's by a relative error of at most 0.009.
Values may be sent and summed in bfloat16 or wider, within the bound.
A program may use at most 64 MiB of HBM per device.

v0:
```python
import math

import jax
import jax.numpy as jnp
from jax import lax
from jax.sharding import PartitionSpec as P


def passed_along(block, axis, distance):
    devices = range(lax.axis_size(axis))
    route = [((i - distance) % len(devices), i) for i in devices]
    return lax.ppermute(block, axis, route)


def lines_of(tile_image):
    return jnp.stack(
        [
            tile_image[..., 0, :],
            tile_image[..., :, -1],
            tile_image[..., -1, :],
            tile_image[..., :, 0],
        ],
        axis=2,
    )


def assemble(tile_image, edge_lines, tile_rules):
    top_line = edge_lines[:, :, 0]
    right_line = edge_lines[:, :, 1]
    bottom_line = edge_lines[:, :, 2]
    left_line = edge_lines[:, :, 3]
    pairs = (
        (top_line[..., 0], left_line[..., 0]),
        (top_line[..., -1], right_line[..., 0]),
        (bottom_line[..., 0], left_line[..., -1]),
        (bottom_line[..., -1], right_line[..., -1]),
    )
    corners = []
    for corner_id in range(4):
        first_value, second_value = pairs[corner_id]
        rule_now = tile_rules[:, corner_id][None, :, None]
        mean_value = (
            (first_value.astype(jnp.float32) + second_value.astype(jnp.float32)) * 0.5
        ).astype(tile_image.dtype)
        corners.append(
            jnp.where(
                rule_now == 0, first_value, jnp.where(rule_now == 1, second_value, mean_value)
            )
        )
    middle = jnp.concatenate(
        [left_line[..., :, None], tile_image, right_line[..., :, None]], axis=-1
    )
    top_row = jnp.concatenate([corners[0][..., None], top_line, corners[1][..., None]], axis=-1)
    bottom_row = jnp.concatenate(
        [corners[2][..., None], bottom_line, corners[3][..., None]], axis=-1
    )
    return jnp.concatenate([top_row[..., None, :], middle, bottom_row[..., None, :]], axis=-2)


def assemble_adjoint(d_padded, tile_rules):
    d_image = d_padded[..., 1:-1, 1:-1]
    d_top = d_padded[..., 0, 1:-1]
    d_bottom = d_padded[..., -1, 1:-1]
    d_left = d_padded[..., 1:-1, 0]
    d_right = d_padded[..., 1:-1, -1]
    first_weight = jnp.where(tile_rules == 0, 1.0, jnp.where(tile_rules == 1, 0.0, 0.5)).astype(
        jnp.float32
    )
    second_weight = 1.0 - first_weight
    corner_grads = (
        d_padded[..., 0, 0],
        d_padded[..., 0, -1],
        d_padded[..., -1, 0],
        d_padded[..., -1, -1],
    )

    def weighted(weight_table, corner_id):
        return weight_table[:, corner_id][None, :, None] * corner_grads[corner_id]

    d_top = (
        d_top.at[..., 0].add(weighted(first_weight, 0)).at[..., -1].add(weighted(first_weight, 1))
    )
    d_left = (
        d_left.at[..., 0]
        .add(weighted(second_weight, 0))
        .at[..., -1]
        .add(weighted(second_weight, 2))
    )
    d_right = (
        d_right.at[..., 0]
        .add(weighted(second_weight, 1))
        .at[..., -1]
        .add(weighted(second_weight, 3))
    )
    d_bottom = (
        d_bottom.at[..., 0]
        .add(weighted(first_weight, 2))
        .at[..., -1]
        .add(weighted(first_weight, 3))
    )
    return (d_image, jnp.stack([d_top, d_right, d_bottom, d_left], axis=2))


def add_lines(d_image, line_grads):
    d_image = d_image.at[..., 0, :].add(line_grads[:, :, 0]).at[..., :, -1].add(line_grads[:, :, 1])
    return d_image.at[..., -1, :].add(line_grads[:, :, 2]).at[..., :, 0].add(line_grads[:, :, 3])


def one_hot(rows, owner, tile_dev, dtype):
    chosen = (rows[:, 0] - owner * tile_dev) * 4 + rows[:, 1]
    return (chosen[:, None] == jnp.arange(tile_dev * 4, dtype=jnp.int32)[None, :]).astype(dtype)


def conv_apply(padded, weights):
    lead = padded.shape[:3]
    row_width = padded.shape[-1]
    side_len = row_width - 2
    out_span = side_len * row_width
    flat_pad = jnp.pad(
        padded.reshape(lead + (row_width * row_width,)), ((0, 0), (0, 0), (0, 0), (0, 2))
    )
    summed = jnp.zeros(lead[:2] + (weights.shape[1], out_span), jnp.float32)
    for tap_id in range(9):
        start_at = tap_id // 3 * row_width + tap_id % 3
        window = lax.slice_in_dim(flat_pad, start_at, start_at + out_span, axis=3)
        summed = summed + jnp.einsum(
            "oc,btcq->btoq", weights[tap_id], window, preferred_element_type=jnp.float32
        )
    return summed.reshape(lead[:2] + (weights.shape[1], side_len, row_width))[
        ..., :side_len
    ].reshape(lead[:2] + (weights.shape[1], side_len * side_len))


def spread_rows(grad, side_len):
    lead = grad.shape[:3]
    squared = grad.reshape(lead + (side_len, side_len))
    return jnp.pad(squared, ((0, 0), (0, 0), (0, 0), (0, 0), (0, 2))).reshape(
        lead + (side_len * (side_len + 2),)
    )


def conv_transpose(grad, weights, side_len):
    lead = grad.shape[:2]
    row_width = side_len + 2
    out_span = side_len * row_width
    full_len = row_width * row_width + 2
    flat_grad = spread_rows(grad, side_len)
    summed = jnp.zeros(lead + (weights.shape[2], full_len), jnp.float32)
    for tap_id in range(9):
        start_at = tap_id // 3 * row_width + tap_id % 3
        placed = jnp.einsum(
            "oc,btoq->btcq", weights[tap_id], flat_grad, preferred_element_type=jnp.float32
        )
        summed = summed + jnp.pad(
            placed, ((0, 0), (0, 0), (0, 0), (start_at, full_len - out_span - start_at))
        )
    return summed[..., : row_width * row_width].reshape(
        lead + (weights.shape[2], row_width, row_width)
    )


def weight_grad(grad, padded):
    lead = padded.shape[:3]
    row_width = padded.shape[-1]
    side_len = row_width - 2
    out_span = side_len * row_width
    flat_grad = spread_rows(grad, side_len)
    flat_pad = jnp.pad(
        padded.reshape(lead + (row_width * row_width,)), ((0, 0), (0, 0), (0, 0), (0, 2))
    )
    taps = []
    for tap_id in range(9):
        start_at = tap_id // 3 * row_width + tap_id % 3
        window = lax.slice_in_dim(flat_pad, start_at, start_at + out_span, axis=3)
        taps.append(
            jnp.einsum("btoq,btcq->oc", flat_grad, window, preferred_element_type=jnp.float32)
        )
    return jnp.stack(taps, axis=0)


def activate(values):
    return jax.nn.gelu(values, approximate=True)


def on_device(inputs, cotangent, conv_one, bias_one, conv_two, bias_two, neighbours, corner_rule):
    batch_dev, tile_dev, channels, pixels = inputs.shape
    side_len = math.isqrt(pixels)
    spaces = lax.axis_size("space")
    hop_dist = spaces // 4
    my_index = lax.axis_index("space")
    offsets = (-1, hop_dist, 1, -hop_dist)
    my_rows = lax.dynamic_slice_in_dim(neighbours, my_index * tile_dev, tile_dev, 0)
    my_rules = lax.dynamic_slice_in_dim(corner_rule, my_index * tile_dev, tile_dev, 0)
    flip_mask = ((my_rows[:, :, 2] == 1) | (my_rows[:, :, 2] == 2))[None, :, :, None, None]
    line_len = channels * side_len

    def fetch_padded(field):
        tile_image = field.reshape(batch_dev, tile_dev, channels, side_len, side_len)
        own_lines = lines_of(tile_image).reshape(batch_dev, tile_dev * 4, line_len)
        collected = []
        for edge_id in range(4):
            offset = offsets[edge_id]
            arrived = passed_along(own_lines, "space", -offset)
            source_device = (my_index + offset) % spaces
            picker = one_hot(my_rows[:, edge_id], source_device, tile_dev, jnp.bfloat16)
            got_lines = jnp.einsum(
                "js,bsk->bjk", picker, arrived, preferred_element_type=jnp.float32
            ).astype(jnp.bfloat16)
            collected.append(got_lines.reshape(batch_dev, tile_dev, channels, side_len))
        edge_lines = jnp.stack(collected, axis=2)
        edge_lines = jnp.where(flip_mask, edge_lines[..., ::-1], edge_lines)
        return assemble(tile_image, edge_lines, my_rules)

    def pull_back(d_padded):
        d_image, d_lines = assemble_adjoint(d_padded, my_rules)
        d_lines = jnp.where(flip_mask, d_lines[..., ::-1], d_lines)
        returned = jnp.zeros((batch_dev, tile_dev * 4, line_len), jnp.float32)
        for edge_id in range(4):
            offset = offsets[edge_id]
            edge_grads = d_lines[:, :, edge_id].reshape(batch_dev, tile_dev, line_len)
            source_device = (my_index + offset) % spaces
            picker = one_hot(my_rows[:, edge_id], source_device, tile_dev, jnp.float32)
            scattered = jnp.einsum(
                "js,bjk->bsk", picker, edge_grads, precision=lax.Precision.HIGHEST
            )
            returned = returned + passed_along(
                scattered.astype(jnp.bfloat16), "space", offset
            ).astype(scattered.dtype)
        line_grads = returned.reshape(batch_dev, tile_dev, 4, channels, side_len)
        return add_lines(d_image, line_grads).reshape(batch_dev, tile_dev, channels, pixels)

    pad_in = fetch_padded(inputs)
    pre_one = conv_apply(pad_in, conv_one) + bias_one[None, None, :, None]
    act_one = activate(pre_one).astype(jnp.bfloat16)
    pad_act = fetch_padded(act_one)
    output = (
        inputs.astype(jnp.float32) + conv_apply(pad_act, conv_two) + bias_two[None, None, :, None]
    ).astype(jnp.bfloat16)
    d_act = pull_back(conv_transpose(cotangent, conv_two, side_len))
    pull_gelu = jax.vjp(activate, pre_one)[1]
    d_pre = pull_gelu(d_act)[0].astype(jnp.bfloat16)
    grad_two = weight_grad(cotangent, pad_act)
    bias_grad_two = jnp.sum(cotangent.astype(jnp.float32), axis=(0, 1, 3))
    grad_one = weight_grad(d_pre, pad_in)
    bias_grad_one = jnp.sum(d_pre.astype(jnp.float32), axis=(0, 1, 3))
    d_in = pull_back(conv_transpose(d_pre, conv_one, side_len))
    grad_in = (cotangent.astype(jnp.float32) + d_in).astype(jnp.bfloat16)
    local_grads = (grad_one, bias_grad_one, grad_two, bias_grad_two)
    summed = lax.psum((local_grads[0], local_grads[1], local_grads[2], local_grads[3]), "space")
    shares = (
        lax.psum_scatter(summed[0], "dp", scatter_dimension=1, tiled=True),
        lax.psum_scatter(summed[1], "dp", scatter_dimension=0, tiled=True),
        lax.psum_scatter(summed[2], "dp", scatter_dimension=1, tiled=True),
        lax.psum_scatter(summed[3], "dp", scatter_dimension=0, tiled=True),
    )
    return (output, grad_in, shares[0], shares[1], shares[2], shares[3])


def solution(mesh):
    placed = (
        P("dp", "space", None, None),
        P("dp", "space", None, None),
        P(),
        P(),
        P(),
        P(),
        P(),
        P(),
    )
    return jax.shard_map(
        on_device,
        mesh=mesh,
        in_specs=placed,
        out_specs=(
            P("dp", "space", None, None),
            P("dp", "space", None, None),
            P(None, "dp", None),
            P("dp"),
            P(None, "dp", None),
            P("dp"),
        ),
        check_vma=False,
    )
```

profile of v0, /device:TPU:24, one launch (start us, length us, event | category | flops | bytes accessed | tf_op | source)
XLA Modules:
  0.0 457.3 jit_solution(7980459896059756995)
XLA Ops:
  7.2 1.8 reshape.1981
  10.8 2.8 collective-permute-start.1
  13.7 5.7 %collective-permute-start.2 = (bf16[1,4,3072]{2,1,0:T(4,128)(2,1)S(1)}, bf16[1,4,3072]{2,1,0:T(4,128)(2,1)S(1)}, u32[]{:S(2)}, u32[]{:S(2)}) collective-permute-start(bf16[1,4,3072]{2,1,0:T(4,128)(2,1)S(1)} %pad_maximum_fusion.4), channel_id=1, source_target_pairs={{1,0},{2,1},{3,2},{4,3},{5,4},{6,5},{7,6},{8,7},{9,8},{10,9},{11,1... | collective-permute-start | bytes 73736 | tf_op jit(solution)/shard_map/ppermute | solution.py:12
  19.4 1.6 collective-permute-start.3
  26.6 2.3 pad_add_fusion.6
  28.8 1.9 reshape.2015
  31.0 2.2 fusion.196
  35.6 1.9 copy.213
  38.2 1.9 copy.215
  40.1 4.8 %slice_multiply_fusion.7 = (f32[1,1,48,1,1]{4,3,2,1,0:T(1,128)S(1)}, f32[1,1,48,1,1]{4,3,2,1,0:T(1,128)S(1)}, f32[1,1,48,1,1]{4,3,2,1,0:T(1,128)S(1)}, f32[1,1,4...) fusion(f32[1,1,48,66,66]{4,3,2,1,0:T(8,128)S(1)} %reshape.2015,, ...), kind=kLoop, calls=%fused_computation.258 | loop fusion | flops 480 | bytes 2716 | tf_op jit(solution)/shard_map/mul | solution.py:78
  48.4 2.1 collective-permute-start.8
  62.4 2.1 copy.211
  66.2 3.3 collective-permute-start.11
  73.0 3.7 pad_maximum_fusion
  76.7 1.9 reshape.1986
  82.4 4.7 %reshape.1996 = f32[1,1,48,64,66]{4,3,2,1,0:T(8,128)} reshape(f32[1,1,48,4224]{3,2,1,0:T(8,128)} %fusion) | data formatting | bytes 1622016 | tf_op jit(solution)/shard_map/reshape | solution.py:129
  87.3 1.8 copy.183
  89.1 3.1 slice_add_fusion.2
  92.2 12.9 %scatter-add.95 = f32[1,1,48,64,64]{4,2,3,1,0:T(8,128)S(1)} dynamic-update-slice(f32[1,1,48,64,64]{4,2,3,1,0:T(8,128)S(1)} %constant_dynamic-update-slice_fusion.8, f32[1,1,48,64,1]{4,2,3,1,0:T(8,128)} %slice_add_fusion.2, s32[]{:T(128)} %constant.613.clone.1, s32[]{:T(128)} %constant.613.clone.1, s32[]{:T(128)} %constant.613.clone.1, s32[]{:T(128)} %constant.613.clone.1, s32[]{:T(128)} %constant.630.clone.1) | dynamic-update-slice | bytes 24580 | tf_op jit(solution)/shard_map/scatter-add | solution.py:105
  105.1 1.8 copy.184
  107.0 2.9 slice_add_fusion.1
  109.8 8.6 %scatter-add.99 = f32[1,1,48,64,64]{4,2,3,1,0:T(8,128)S(1)} dynamic-update-slice(f32[1,1,48,64,64]{4,2,3,1,0:T(8,128)S(1)} %fusion.55, f32[1,1,48,64,1]{4,2,3,1,0:T(8,128)} %slice_add_fusion.1, s32[]{:T(128)} %constant.613.clone.1, s32[]{:T(128)} %constant.613.clone.1, s32[]{:T(128)} %constant.613.clone.1, s32[]{:T(128)} %constant.613.clone.1, s32[]{:T(128)} %constant.613.clone.1) | dynamic-update-slice | bytes 24580 | tf_op jit(solution)/shard_map/scatter-add | solution.py:106
  118.5 4.2 convert_reduce_fusion
  127.6 2.3 pad_add_fusion
  129.9 1.9 reshape.2026
  132.8 4.7 %slice_multiply_fusion.3 = (f32[1,1,48,1,1]{4,3,2,1,0:T(1,128)S(1)}, f32[1,1,48,1,1]{4,3,2,1,0:T(1,128)S(1)}, f32[1,1,48,1,1]{4,3,2,1,0:T(1,128)S(1)}, f32[1,1,4...) fusion(f32[1,1,48,66,66]{4,3,2,1,0:T(8,128)S(1)} %reshape.2026,, ...), kind=kLoop, calls=%fused_computation.254 | loop fusion | flops 480 | bytes 2716 | tf_op jit(solution)/shard_map/mul | solution.py:78
  137.5 2.2 fusion.194
  141.1 1.8 copy.160
  143.0 1.8 copy.161
  145.3 6.2 %collective-permute-start.6 = (bf16[1,4,3072]{2,1,0:T(4,128)(2,1)S(1)}, bf16[1,4,3072]{2,1,0:T(4,128)(2,1)}, u32[]{:S(2)}, u32[]{:S(2)}) collective-permute-start(bf16[1,4,3072]{2,1,0:T(4,128)(2,1)S(1)} %pad_maximum_fusion.5), channel_id=1, source_target_pairs={{1,0},{2,1},{3,2},{4,3},{5,4},{6,5},{7,6},{8,7},{9,8},{10,9},{11,1... | collective-permute-start | bytes 73736 | tf_op jit(solution)/shard_map/ppermute | solution.py:12
  153.1 1.9 copy.218
  155.0 1.9 copy.220
  168.1 1.6 slice.1424
  169.7 3.2 copy.216
  174.9 3.2 collective-permute-start.15
  183.0 2.1 pad_maximum_fusion.1
  186.3 2.1 reshape.2001
  190.7 1.8 copy.203
  192.5 8.2 %scatter-add.114 = f32[1,1,48,64,64]{3,2,4,1,0:T(8,128)S(1)} dynamic-update-slice(f32[1,1,48,64,64]{3,2,4,1,0:T(8,128)S(1)} %copy-done.1, f32[1,1,48,1,64]{3,2,4,1,0:T(8,128)} %copy.203, s32[]{:T(128)} %constant.613.clone.1, s32[]{:T(128)} %constant.613.clone.1, s32[]{:T(128)} %constant.613.clone.1, s32[]{:T(128)} %constant.613.clone.1, s32[]{:T(128)} %constant.613.clone.1) | dynamic-update-slice | bytes 24580 | tf_op jit(solution)/shard_map/scatter-add | solution.py:105
  200.7 1.8 copy.204
  202.6 3.1 slice_add_fusion
  205.6 12.9 %scatter-add.116 = f32[1,1,48,64,64]{3,2,4,1,0:T(8,128)S(1)} dynamic-update-slice(f32[1,1,48,64,64]{3,2,4,1,0:T(8,128)S(1)} %fusion.49, f32[1,1,48,1,64]{3,2,4,1,0:T(8,128)} %slice_add_fusion, s32[]{:T(128)} %constant.613.clone.1, s32[]{:T(128)} %constant.613.clone.1, s32[]{:T(128)} %constant.613.clone.1, s32[]{:T(128)} %constant.630.clone.1, s32[]{:T(128)} %constant.613.clone.1) | dynamic-update-slice | bytes 24580 | tf_op jit(solution)/shard_map/scatter-add | solution.py:106
  218.6 1.8 copy.205
  220.4 1.9 reshape.2036
  228.7 3.5 reshape.2011
  235.0 15.9 %all-reduce.27 = (f32[48]{0:T(128)S(1)}, f32[48]{0:T(128)S(1)}) all-reduce(f32[48]{0:T(128)S(1)} %get-tuple-element.310, f32[48]{0:T(128)S(1)} %get-tuple-element.341), channel_id=3, replica_groups=mesh['dp'=8,'space'=32] {'dp'}, use_global_device_ids=true, to_apply=%region_4.5.clone | all-reduce | flops 96 | bytes 768
  251.0 58.0 %all-reduce.31.cloned.1.call-done = (f32[9,48,48]{2,1,0:T(8,128)}, f32[9,48,48]{2,1,0:T(8,128)}) async-done(((f32[9,48,48]{2,1,0:T(8,128)}, f32[9,48,48]{2,1,0:T(8,128)}), (f32[9,48,48]{2,1,0:T(8,128)}, f32[9,48,48]{2,1,0:T(8,128)})) %all-reduce.31.cloned.1.call-update) | async-done | bytes 165904
  310.8 139.4 %all-reduce.26 = (f32[9,6,48]{2,1,0:T(8,128)}, f32[6]{0:T(128)}, f32[9,6,48]{2,1,0:T(8,128)}, f32[6]{0:T(128)}) all-reduce(f32[9,6,48]{2,1,0:T(8,128)S(1)} %constant_dynamic-slice_fusion.7, f32[6]{0:T(128)S(1)} %dynamic-slice.195, f32[9,6,48]{2,1,0:T(8,128)S(1)} %constant_dynamic-slice_fusion.6, ...), channel_id=1, replica_groups=mesh['dp'=8,'space'=32] {'space'}, use_global_device_ids=true, to_apply=%region_0.1 | all-reduce | flops 5196 | bytes 41568 | tf_op jit(solution)/shard_map/psum | solution.py:249
  (277 shorter events, 65.9 us)
Async XLA Ops:
  7.2 13.9 %copy-start.6 = (bf16[1,1,48,4096]{3,2,1,0:T(8,128)(2,1)S(1)}, bf16[1,1,48,4096]{3,2,1,0:T(8,128)(2,1)}, u32[]{:S(2)}) copy-start(bf16[1,1,48,4096]{3,2,1,0:T(8,128)(2,1)} %param.57) | copy-start | bytes 1179652
  7.2 301.9 %all-reduce.31.cloned.1.call-start = ((), (), s32[]{:S(2)}) async-start(), calls=%async_computation | async-start | bytes 884736
  10.7 54.9 %collective-permute-start = (bf16[1,4,3072]{2,1,0:T(4,128)(2,1)S(1)}, bf16[1,4,3072]{2,1,0:T(4,128)(2,1)S(1)}, u32[]{:S(2)}, u32[]{:S(2)}) collective-permute-start(bf16[1,4,3072]{2,1,0:T(4,128)(2,1)S(1)} %pad_maximum_fusion.4), channel_id=1, source_target_pairs={{31,0},{0,1},{1,2},{2,3},{3,4},{4,5},{5,6},{6,7},{7,8},{8,9},{9,10... | collective-permute-start | bytes 73736 | tf_op jit(solution)/shard_map/ppermute | solution.py:12
  10.8 55.0 %collective-permute-start.1 = (bf16[1,4,3072]{2,1,0:T(4,128)(2,1)S(1)}, bf16[1,4,3072]{2,1,0:T(4,128)(2,1)S(1)}, u32[]{:S(2)}, u32[]{:S(2)}) collective-permute-start(bf16[1,4,3072]{2,1,0:T(4,128)(2,1)S(1)} %pad_maximum_fusion.4), channel_id=1, source_target_pairs={{8,0},{9,1},{10,2},{11,3},{12,4},{13,5},{14,6},{15,7},{16,8},{17,9... | collective-permute-start | bytes 73736 | tf_op jit(solution)/shard_map/ppermute | solution.py:12
  13.7 52.5 %collective-permute-start.2 = (bf16[1,4,3072]{2,1,0:T(4,128)(2,1)S(1)}, bf16[1,4,3072]{2,1,0:T(4,128)(2,1)S(1)}, u32[]{:S(2)}, u32[]{:S(2)}) collective-permute-start(bf16[1,4,3072]{2,1,0:T(4,128)(2,1)S(1)} %pad_maximum_fusion.4), channel_id=1, source_target_pairs={{1,0},{2,1},{3,2},{4,3},{5,4},{6,5},{7,6},{8,7},{9,8},{10,9},{11,1... | collective-permute-start | bytes 73736 | tf_op jit(solution)/shard_map/ppermute | solution.py:12
  19.4 50.4 %collective-permute-start.3 = (bf16[1,4,3072]{2,1,0:T(4,128)(2,1)S(1)}, bf16[1,4,3072]{2,1,0:T(4,128)(2,1)S(1)}, u32[]{:S(2)}, u32[]{:S(2)}) collective-permute-start(bf16[1,4,3072]{2,1,0:T(4,128)(2,1)S(1)} %pad_maximum_fusion.4), channel_id=1, source_target_pairs={{24,0},{25,1},{26,2},{27,3},{28,4},{29,5},{30,6},{31,7},{0,8},{1,9... | collective-permute-start | bytes 73736 | tf_op jit(solution)/shard_map/ppermute | solution.py:12
  21.9 1.4 copy-start.9
  31.0 2.2 copy-start.13
  31.0 3.4 copy-start.14
  48.4 38.7 %collective-permute-start.8 = (bf16[1,4,3072]{2,1,0:T(4,128)(2,1)S(1)}, bf16[1,4,3072]{2,1,0:T(4,128)(2,1)S(1)}, u32[]{:S(2)}, u32[]{:S(2)}) collective-permute-start(bf16[1,4,3072]{2,1,0:T(4,128)(2,1)S(1)} %fusion.38), channel_id=1, source_target_pairs={{1,0},{2,1},{3,2},{4,3},{5,4},{6,5},{7,6},{8,7},{9,8},{10,9},{11,1... | collective-permute-start | bytes 73736 | tf_op jit(solution)/shard_map/ppermute | solution.py:12
  62.3 2.1 copy-start.17
  65.6 21.4 %collective-permute-start.9 = (bf16[1,4,3072]{2,1,0:T(4,128)(2,1)S(1)}, bf16[1,4,3072]{2,1,0:T(4,128)(2,1)S(1)}, u32[]{:S(2)}, u32[]{:S(2)}) collective-permute-start(bf16[1,4,3072]{2,1,0:T(4,128)(2,1)S(1)} %fusion.39), channel_id=1, source_target_pairs={{24,0},{25,1},{26,2},{27,3},{28,4},{29,5},{30,6},{31,7},{0,8},{1,9... | collective-permute-start | bytes 73736 | tf_op jit(solution)/shard_map/ppermute | solution.py:12
  65.8 21.2 %collective-permute-start.10 = (bf16[1,4,3072]{2,1,0:T(4,128)(2,1)S(1)}, bf16[1,4,3072]{2,1,0:T(4,128)(2,1)S(1)}, u32[]{:S(2)}, u32[]{:S(2)}) collective-permute-start(bf16[1,4,3072]{2,1,0:T(4,128)(2,1)S(1)} %fusion.40), channel_id=1, source_target_pairs={{31,0},{0,1},{1,2},{2,3},{3,4},{4,5},{5,6},{6,7},{7,8},{8,9},{9,10... | collective-permute-start | bytes 73736 | tf_op jit(solution)/shard_map/ppermute | solution.py:12
  66.2 20.9 %collective-permute-start.11 = (bf16[1,4,3072]{2,1,0:T(4,128)(2,1)S(1)}, bf16[1,4,3072]{2,1,0:T(4,128)(2,1)S(1)}, u32[]{:S(2)}, u32[]{:S(2)}) collective-permute-start(bf16[1,4,3072]{2,1,0:T(4,128)(2,1)S(1)} %fusion.41), channel_id=1, source_target_pairs={{8,0},{9,1},{10,2},{11,3},{12,4},{13,5},{14,6},{15,7},{16,8},{17,9... | collective-permute-start | bytes 73736 | tf_op jit(solution)/shard_map/ppermute | solution.py:12
  73.0 5.6 %copy-start.8 = (bf16[9,48,48]{2,1,0:T(8,128)(2,1)S(1)}, bf16[9,48,48]{2,1,0:T(8,128)(2,1)}, u32[]{:S(2)}) copy-start(bf16[9,48,48]{2,1,0:T(8,128)(2,1)} %param.58) | copy-start | bytes 124420
  87.3 1.8 copy-start
  109.8 8.7 %copy-start.15 = (f32[48]{0:T(128)S(1)}, f32[48]{0:T(128)}, u32[]{:S(2)}) copy-start(f32[48]{0:T(128)} %param.59) | copy-start | bytes 580
  137.5 2.2 copy-start.2
  145.1 27.8 %collective-permute-start.5 = (bf16[1,4,3072]{2,1,0:T(4,128)(2,1)S(1)}, bf16[1,4,3072]{2,1,0:T(4,128)(2,1)}, u32[]{:S(2)}, u32[]{:S(2)}) collective-permute-start(bf16[1,4,3072]{2,1,0:T(4,128)(2,1)S(1)} %pad_maximum_fusion.5), channel_id=1, source_target_pairs={{8,0},{9,1},{10,2},{11,3},{12,4},{13,5},{14,6},{15,7},{16,8},{17,9... | collective-permute-start | bytes 73736 | tf_op jit(solution)/shard_map/ppermute | solution.py:12
  145.2 28.6 %collective-permute-start.4 = (bf16[1,4,3072]{2,1,0:T(4,128)(2,1)S(1)}, bf16[1,4,3072]{2,1,0:T(4,128)(2,1)}, u32[]{:S(2)}, u32[]{:S(2)}) collective-permute-start(bf16[1,4,3072]{2,1,0:T(4,128)(2,1)S(1)} %pad_maximum_fusion.5), channel_id=1, source_target_pairs={{31,0},{0,1},{1,2},{2,3},{3,4},{4,5},{5,6},{6,7},{7,8},{8,9},{9,10... | collective-permute-start | bytes 73736 | tf_op jit(solution)/shard_map/ppermute | solution.py:12
  145.3 29.6 %collective-permute-start.6 = (bf16[1,4,3072]{2,1,0:T(4,128)(2,1)S(1)}, bf16[1,4,3072]{2,1,0:T(4,128)(2,1)}, u32[]{:S(2)}, u32[]{:S(2)}) collective-permute-start(bf16[1,4,3072]{2,1,0:T(4,128)(2,1)S(1)} %pad_maximum_fusion.5), channel_id=1, source_target_pairs={{1,0},{2,1},{3,2},{4,3},{5,4},{6,5},{7,6},{8,7},{9,8},{10,9},{11,1... | collective-permute-start | bytes 73736 | tf_op jit(solution)/shard_map/ppermute | solution.py:12
  151.5 27.7 %collective-permute-start.7 = (bf16[1,4,3072]{2,1,0:T(4,128)(2,1)S(1)}, bf16[1,4,3072]{2,1,0:T(4,128)(2,1)S(1)}, u32[]{:S(2)}, u32[]{:S(2)}) collective-permute-start(bf16[1,4,3072]{2,1,0:T(4,128)(2,1)S(1)} %pad_maximum_fusion.5), channel_id=1, source_target_pairs={{24,0},{25,1},{26,2},{27,3},{28,4},{29,5},{30,6},{31,7},{0,8},{1,9... | collective-permute-start | bytes 73736 | tf_op jit(solution)/shard_map/ppermute | solution.py:12
  159.0 31.4 %collective-permute-start.12 = (bf16[1,4,3072]{2,1,0:T(4,128)(2,1)S(1)}, bf16[1,4,3072]{2,1,0:T(4,128)(2,1)S(1)}, u32[]{:S(2)}, u32[]{:S(2)}) collective-permute-start(bf16[1,4,3072]{2,1,0:T(4,128)(2,1)S(1)} %fusion.42), channel_id=1, source_target_pairs={{1,0},{2,1},{3,2},{4,3},{5,4},{6,5},{7,6},{8,7},{9,8},{10,9},{11,1... | collective-permute-start | bytes 73736 | tf_op jit(solution)/shard_map/ppermute | solution.py:12
  172.9 10.0 %copy-start.3 = (bf16[1,1,48,64,64]{4,2,3,1,0:T(8,128)(2,1)S(1)}, bf16[1,1,48,64,64]{4,2,3,1,0:T(8,128)(2,1)}, u32[]{:S(2)}) copy-start(bf16[1,1,48,64,64]{4,2,3,1,0:T(8,128)(2,1)} %get-tuple-element.336) | copy-start | bytes 1179652
  172.9 17.5 %collective-permute-start.13 = (bf16[1,4,3072]{2,1,0:T(4,128)(2,1)S(1)}, bf16[1,4,3072]{2,1,0:T(4,128)(2,1)S(1)}, u32[]{:S(2)}, u32[]{:S(2)}) collective-permute-start(bf16[1,4,3072]{2,1,0:T(4,128)(2,1)S(1)} %fusion.43), channel_id=1, source_target_pairs={{24,0},{25,1},{26,2},{27,3},{28,4},{29,5},{30,6},{31,7},{0,8},{1,9... | collective-permute-start | bytes 73736 | tf_op jit(solution)/shard_map/ppermute | solution.py:12
  173.9 16.5 %collective-permute-start.14 = (bf16[1,4,3072]{2,1,0:T(4,128)(2,1)S(1)}, bf16[1,4,3072]{2,1,0:T(4,128)(2,1)S(1)}, u32[]{:S(2)}, u32[]{:S(2)}) collective-permute-start(bf16[1,4,3072]{2,1,0:T(4,128)(2,1)S(1)} %fusion.44), channel_id=1, source_target_pairs={{31,0},{0,1},{1,2},{2,3},{3,4},{4,5},{5,6},{6,7},{7,8},{8,9},{9,10... | collective-permute-start | bytes 73736 | tf_op jit(solution)/shard_map/ppermute | solution.py:12
  174.9 15.5 %collective-permute-start.15 = (bf16[1,4,3072]{2,1,0:T(4,128)(2,1)S(1)}, bf16[1,4,3072]{2,1,0:T(4,128)(2,1)S(1)}, u32[]{:S(2)}, u32[]{:S(2)}) collective-permute-start(bf16[1,4,3072]{2,1,0:T(4,128)(2,1)S(1)} %fusion.45), channel_id=1, source_target_pairs={{8,0},{9,1},{10,2},{11,3},{12,4},{13,5},{14,6},{15,7},{16,8},{17,9... | collective-permute-start | bytes 73736 | tf_op jit(solution)/shard_map/ppermute | solution.py:12
  185.1 3.3 copy-start.10
  190.7 1.8 copy-start.1
  220.4 1.9 copy-start.11
  223.7 1.4 copy-start.4
  225.1 0.7 copy-start.12
  232.2 1.0 copy-start.5
  232.2 1.0 copy-start.16
  232.7 1.3 copy-start.7
Sparse Core Ops, SparseCore 0:
  232.9 76.1 all-reduce.30
where the time goes:
time: 463 us; the launch traced here: 457 us
  blocking collectives  155 us (33%)
  local copies, waits for them, and re-layouts  121 us (26%)
  waiting for transfers between devices  58.1 us (13%)
  other arithmetic  40.3 us (9%)
  matrix products  29.1 us (6%)
  starting transfers between devices  27.4 us (6%)
  between operations  25.8 us (6%)
    psum x1, blocking collectives, on_device(): lax.psum((local_grads[0], local_grads[1], local_grads[2], local_grads[3])...  139 us
    unnamed x2, waiting for transfers between devices  58 us
    ppermute x16, starting transfers between devices, passed_along(): return lax.ppermute(block, axis, route)  27.3 us
    scatter-add x3, local copies, waits for them, and re-layouts, add_lines(): d_image.at[..., -1, :].add(line_grads[:, :, 2]).at[..., :, 0]  23.4 us
    scatter-add x3, local copies, waits for them, and re-layouts, add_lines(): d_image.at[..., 0, :].add(line_grads[:, :, 0]).at[..., :, -1]  21.1 us
    unnamed x54, local copies, waits for them, and re-layouts  16.3 us
    unnamed x1, blocking collectives  15.9 us
    dot_general x18, matrix products, weight_grad(): jnp.einsum('btoq,btcq->oc', flat_grad, window, preferred_element_type=jnp...  12 us
  transfers between devices with their start and end apart: 17, of which 1 were waited for; matrix products, arithmetic and copies ran while one was open for 19% of the time, Pallas kernels for 0%

commit v1 on v0

v1 whole, which is shorter than its diff:
```python
import functools
import math

import jax
import jax.numpy as jnp
from jax import lax
from jax.experimental import pallas as pl
from jax.experimental.pallas import tpu as pltpu
from jax.sharding import PartitionSpec as P

MESH = pl.DeviceIdType.MESH
F32 = jnp.float32
BF16 = jnp.bfloat16
LANES = 128
CH = 48
SIDE = 64
GROUPS = 32
EXTRA = 32
WIDE = (GROUPS + 1) * LANES
K3 = 3 * CH
ROOT = math.sqrt(2.0 / math.pi)


def grp(v):
    return slice(v * LANES, (v + 1) * LANES)


def roll(values, shift):
    shift = shift % LANES
    return pltpu.roll(values, shift, 1) if shift else values


def dot(a, b, dims):
    return lax.dot_general(a, b, (dims, ((), ())), preferred_element_type=F32)


def line_lane(edge, q):
    odd = (q & 1) == 1
    col_left = jnp.where(odd, q + 63, q)
    col_right = jnp.where(odd, (q + 126) & 127, q + 63)
    return jnp.where(
        edge == 0, q, jnp.where(edge == 2, q + 64, jnp.where(edge == 3, col_left, col_right))
    )


def halo_index(edge, lane):
    if edge == 0:
        return jnp.where(lane >= 64, lane - 64, -1000)
    if edge == 2:
        return jnp.where(lane < 64, lane, -1000)
    even = (lane & 1) == 0
    if edge == 3:
        return jnp.where(even, jnp.where(lane < 64, lane, lane - 63), -1000)
    return jnp.where(even, -1000, jnp.where(lane == 127, 1, jnp.where(lane >= 63, lane - 63, lane + 2)))


def mover(edge, line, rotation):
    lane = lax.broadcasted_iota(jnp.int32, (8, LANES), 1)
    q = halo_index(edge, lane)
    turned = jnp.where((rotation == 1) | (rotation == 2), 63 - q, q)
    source = jnp.where(q < 0, -1, line_lane(line, turned))
    rows = lax.broadcasted_iota(jnp.int32, (LANES, LANES), 0)
    return jnp.where(rows == jnp.broadcast_to(source[0:1], (LANES, LANES)), 1.0, 0.0).astype(BF16)


def column(vector):
    rows = lax.broadcasted_iota(jnp.int32, (CH, CH), 0)
    cols = lax.broadcasted_iota(jnp.int32, (CH, CH), 1)
    spread = jnp.broadcast_to(vector, (CH, CH))
    return jnp.sum(jnp.where(rows == cols, spread, 0.0), axis=1, keepdims=True)


def block_kernel(
    n_dp,
    n_space,
    x_hbm,
    g_hbm,
    w1_ref,
    b1_ref,
    w2_ref,
    b2_ref,
    nb_ref,
    rule_ref,
    out_hbm,
    gin_hbm,
    gw1_ref,
    gb1_ref,
    gw2_ref,
    gb2_ref,
    x_v,
    g_v,
    act_v,
    dpre_v,
    out_v,
    gin_v,
    slope_v,
    ex_v,
    ea_v,
    gs2_v,
    gs1_v,
    y_fwd,
    y_two,
    y_one,
    fwd_send,
    fwd_recv,
    adj_send,
    adj_recv,
    part_send,
    buf_a,
    buf_b,
    buf_c,
    load_sem,
    store_sem,
    halo_ssem,
    halo_rsem,
    a_ssem,
    a_rsem,
    b_ssem,
    b_rsem,
    c_ssem,
    c_rsem,
):
    hop = n_space // 4
    n_c = 4
    n_b = n_space // n_c
    rows_dev = CH // n_dp
    rows_pad = (rows_dev + 7) // 8 * 8
    me = lax.axis_index("space")
    my_dp = lax.axis_index("dp")
    my_b = lax.rem(me, n_b)
    my_c = lax.div(me, n_b)
    offsets = (-1, hop, 1, -hop)
    toward = [lax.rem(me + off + n_space, n_space) for off in offsets]
    reader = [lax.rem(me - off + n_space, n_space) for off in offsets]
    peers_a = [lax.rem(my_dp + s, n_dp) for s in range(1, n_dp)]
    peers_b = [my_c * n_b + lax.rem(my_b + s, n_b) for s in range(1, n_b)]
    peers_c = [lax.rem(my_c + s, n_c) * n_b + my_b for s in range(1, n_c)]

    load_x = pltpu.make_async_copy(x_hbm.at[0, 0], x_v, load_sem.at[0])
    load_g = pltpu.make_async_copy(g_hbm.at[0, 0], g_v, load_sem.at[1])
    load_x.start()
    load_g.start()

    barrier = pltpu.get_barrier_semaphore()
    for dev in toward:
        pl.semaphore_signal(barrier, inc=1, device_id={"space": dev}, device_id_type=MESH)
    for dev in peers_a:
        pl.semaphore_signal(barrier, inc=1, device_id={"dp": dev}, device_id_type=MESH)
    for dev in peers_b + peers_c:
        pl.semaphore_signal(barrier, inc=1, device_id={"space": dev}, device_id_type=MESH)

    lane = lax.broadcasted_iota(jnp.int32, (CH, LANES), 1)
    low = lane < 64
    first_col = (lane & 63) == 0
    last_col = (lane & 63) == 63
    edge_col = first_col | last_col
    zero = jnp.zeros((CH, LANES), F32)

    def remote(src, dst, ssem, rsem, device):
        return pltpu.make_async_remote_copy(
            src_ref=src,
            dst_ref=dst,
            send_sem=ssem,
            recv_sem=rsem,
            device_id=device,
            device_id_type=MESH,
        )

    def halo_copy(sends, recvs, slot, edge, dev):
        at = slot * 4 + edge
        return remote(
            sends.at[edge], recvs.at[edge], halo_ssem.at[at], halo_rsem.at[at], {"space": dev}
        )

    fwd_line = [nb_ref[reader[e], e, 1] for e in range(4)]
    fwd_turn = [nb_ref[reader[e], e, 2] for e in range(4)]
    own_line = [nb_ref[me, e, 1] for e in range(4)]
    own_turn = [nb_ref[me, e, 2] for e in range(4)]
    fwd_movers = [mover(e, fwd_line[e], fwd_turn[e]) for e in range(4)]

    def forward_messages(group_of, sends):
        rows = jnp.where(low, group_of(0), group_of(GROUPS - 1))
        cols = [zero, zero, zero, zero]
        for v in range(GROUPS):
            cols[v % 4] = cols[v % 4] + roll(jnp.where(edge_col, group_of(v), 0.0), 2 * v)
        cols = (cols[0] + cols[1]) + (cols[2] + cols[3])
        for e in range(4):
            source = jnp.where((fwd_line[e] & 1) == 1, cols, rows).astype(BF16)
            sends[e] = dot(source, fwd_movers[e], ((1,), (0,))).astype(BF16)

    def corner_seconds(spread):
        return jnp.where(low, roll(spread, 2), roll(spread, 64))

    rules = [rule_ref[me, c] for c in range(4)]
    rule_at = jnp.where(
        lane == 64,
        rules[0],
        jnp.where(lane == 127, rules[1], jnp.where(lane == 0, rules[2], rules[3])),
    )

    def fill_padded(group_of, recvs, padded):
        spread = recvs[1].astype(F32) + recvs[3].astype(F32)
        outer = recvs[0].astype(F32) + recvs[2].astype(F32)
        second = corner_seconds(spread)
        mean = ((outer + second) * 0.5).astype(BF16).astype(F32)
        corners = jnp.where(rule_at == 0, outer, jnp.where(rule_at == 1, second, mean))
        for v in range(GROUPS + 1):
            here = outer if v == EXTRA else group_of(v)
            sides = corners if v == EXTRA else roll(spread, -2 * v)
            padded[0:CH, grp(v)] = jnp.where(first_col, sides, roll(here, 1)).astype(BF16)
            padded[CH : 2 * CH, grp(v)] = here.astype(BF16)
            padded[2 * CH : K3, grp(v)] = jnp.where(last_col, sides, roll(here, -1)).astype(BF16)
        padded[K3 : K3 + 16, :] = jnp.ones((16, WIDE), BF16)

    def stacked(w_ref):
        return jnp.concatenate(
            [
                jnp.concatenate([w_ref[3 * a + b] for b in range(3)], axis=1)
                for a in range(3)
            ],
            axis=0,
        )

    def conv(weights, padded, y_ref):
        y_ref[...] = dot(weights, padded[0:K3, :], ((1,), (0,)))

    def conv_group(y_ref, v):
        prev = EXTRA if v == 0 else v - 1
        both = jnp.where(
            low,
            y_ref[0:CH, grp(v)] + y_ref[2 * CH : K3, grp(v + 1)],
            y_ref[2 * CH : K3, grp(v)] + y_ref[0:CH, grp(prev)],
        )
        return y_ref[CH : 2 * CH, grp(v)] + roll(both, 64)

    def stack_rows(grad_v, gs_ref):
        turned = None
        for v in range(GROUPS + 1):
            before = turned
            if v == EXTRA:
                gs_ref[CH : 2 * CH, grp(v)] = zero.astype(BF16)
                gs_ref[2 * CH : K3, grp(v)] = jnp.where(low, before, 0.0).astype(BF16)
                gs_ref[0:CH, grp(v - 1)] = jnp.where(low, before, 0.0).astype(BF16)
                gs_ref[0:CH, grp(v)] = jnp.where(
                    low, 0.0, roll(grad_v[:, grp(0)].astype(F32), 64)
                ).astype(BF16)
                continue
            here = grad_v[:, grp(v)]
            turned = roll(here.astype(F32), 64)
            gs_ref[CH : 2 * CH, grp(v)] = here
            gs_ref[2 * CH : K3, grp(v)] = jnp.where(
                low, 0.0 if v == 0 else before, turned
            ).astype(BF16)
            if v > 0:
                gs_ref[0:CH, grp(v - 1)] = jnp.where(low, before, turned).astype(BF16)

    def transpose_conv(weights, gs_ref, y_ref):
        y_ref[...] = dot(weights, gs_ref[...], ((0,), (0,)))

    def inner_group(y_ref, v):
        left = jnp.where(last_col, 0.0, roll(y_ref[0:CH, grp(v)], -1))
        right = jnp.where(first_col, 0.0, roll(y_ref[2 * CH : K3, grp(v)], 1))
        return y_ref[CH : 2 * CH, grp(v)] + (left + right)

    first_weight = jnp.where(rule_at == 0, 1.0, jnp.where(rule_at == 1, 0.0, 0.5))

    def adjoint_messages(y_ref, sends):
        def sides(v):
            return jnp.where(
                edge_col,
                jnp.where(last_col, y_ref[2 * CH : K3, grp(v)], y_ref[0:CH, grp(v)]),
                0.0,
            )

        cols = [zero, zero, zero, zero]
        for v in range(GROUPS):
            cols[v % 4] = cols[v % 4] + roll(sides(v), 2 * v)
        corners = sides(EXTRA)
        firsts = first_weight * corners
        seconds = corners - firsts
        cols = (
            (cols[0] + cols[1])
            + (cols[2] + cols[3])
            + roll(jnp.where(low, seconds, 0.0), -2)
            + roll(jnp.where(low, 0.0, seconds), 64)
        ).astype(BF16)
        rows = (inner_group(y_ref, EXTRA) + firsts).astype(BF16)
        for e in range(4):
            move = mover(e, own_line[e], own_turn[e])
            source = cols if e % 2 else rows
            sends[e] = dot(source, move, ((1,), (1,))).astype(BF16)

    def returned_lines(recvs):
        rows, cols = zero, zero
        for e in range(4):
            message = recvs[e].astype(F32)
            is_col = (fwd_line[e] & 1) == 1
            rows = rows + jnp.where(is_col, 0.0, message)
            cols = cols + jnp.where(is_col, message, 0.0)
        return rows, cols

    def pulled_back(y_ref, rows, cols, v):
        total = inner_group(y_ref, v) + jnp.where(edge_col, roll(cols, -2 * v), 0.0)
        if v == 0:
            total = total + jnp.where(low, rows, 0.0)
        if v == GROUPS - 1:
            total = total + jnp.where(low, 0.0, rows)
        return total

    def put_part(grads, main, rest_shift):
        rest = grads[:, LANES:]
        for d in range(n_dp):
            for a in range(3):
                at = a * CH + d * rows_dev
                part_send[d, main, a * rows_pad : a * rows_pad + rows_dev, :] = grads[
                    at : at + rows_dev, 0:LANES
                ]
                part_send[
                    d, 2, a * rows_pad : a * rows_pad + rows_dev, rest_shift : rest_shift + 32
                ] = rest[at : at + rows_dev]

    part_send[...] = jnp.zeros(part_send.shape, F32)
    load_x.wait()

    def x_group(v):
        return x_v[:, grp(v)].astype(F32)

    forward_messages(x_group, fwd_send.at[0])
    pl.semaphore_wait(barrier, 4 + len(peers_a) + len(peers_b) + len(peers_c))
    in_fwd = [halo_copy(fwd_send.at[0], fwd_recv.at[0], 0, e, reader[e]) for e in range(4)]
    for copy in in_fwd:
        copy.start()

    load_g.wait()
    w_two = stacked(w2_ref)
    stack_rows(g_v, gs2_v)
    transpose_conv(w_two, gs2_v, y_two)
    adjoint_messages(y_two, adj_send.at[0])
    two_adj = [halo_copy(adj_send.at[0], adj_recv.at[0], 1, e, toward[e]) for e in range(4)]
    for copy in two_adj:
        copy.start()

    w_one = stacked(w1_ref)
    bias_one = jnp.broadcast_to(column(b1_ref[...].reshape(1, CH)), (CH, LANES))
    bias_two = jnp.broadcast_to(column(b2_ref[...].reshape(1, CH)), (CH, LANES))
    for copy in in_fwd:
        copy.wait_recv()
    fill_padded(x_group, fwd_recv.at[0], ex_v)
    conv(w_one, ex_v, y_fwd)
    for v in range(GROUPS):
        pre = conv_group(y_fwd, v) + bias_one
        square = pre * pre
        th = jnp.tanh(ROOT * (pre + 0.044715 * (square * pre)))
        cdf = 0.5 * (1.0 + th)
        act_v[:, grp(v)] = (pre * cdf).astype(BF16)
        slope_v[:, grp(v)] = cdf + (0.5 * pre) * (1.0 - th * th) * (
            ROOT * (1.0 + (3.0 * 0.044715) * square)
        )

    def act_group(v):
        return act_v[:, grp(v)].astype(F32)

    forward_messages(act_group, fwd_send.at[1])
    act_fwd = [halo_copy(fwd_send.at[1], fwd_recv.at[1], 2, e, reader[e]) for e in range(4)]
    for copy in act_fwd:
        copy.start()

    for copy in two_adj:
        copy.wait_recv()
    rows, cols = returned_lines(adj_recv.at[0])
    for v in range(GROUPS):
        dpre_v[:, grp(v)] = (pulled_back(y_two, rows, cols, v) * slope_v[:, grp(v)]).astype(BF16)
    stack_rows(dpre_v, gs1_v)
    transpose_conv(w_one, gs1_v, y_one)
    adjoint_messages(y_one, adj_send.at[1])
    one_adj = [halo_copy(adj_send.at[1], adj_recv.at[1], 3, e, toward[e]) for e in range(4)]
    for copy in one_adj:
        copy.start()
    put_part(dot(gs1_v[...], ex_v[...], ((1,), (1,))), 0, 0)

    for copy in act_fwd:
        copy.wait_recv()
    fill_padded(act_group, fwd_recv.at[1], ea_v)
    put_part(dot(gs2_v[...], ea_v[...], ((1,), (1,))), 1, 32)
    dp_copies = [
        remote(
            part_send.at[dev], buf_a.at[my_dp], a_ssem.at[s], a_rsem.at[s], {"dp": dev}
        )
        for s, dev in enumerate(peers_a)
    ]
    for copy in dp_copies:
        copy.start()
    buf_a[my_dp] = part_send[my_dp]

    conv(w_two, ea_v, y_fwd)
    for v in range(GROUPS):
        out_v[:, grp(v)] = (x_group(v) + conv_group(y_fwd, v) + bias_two).astype(BF16)
    store_out = pltpu.make_async_copy(out_v, out_hbm.at[0, 0], store_sem.at[0])
    store_out.start()

    for copy in one_adj:
        copy.wait_recv()
    rows, cols = returned_lines(adj_recv.at[1])
    for v in range(GROUPS):
        gin_v[:, grp(v)] = (
            g_v[:, grp(v)].astype(F32) + pulled_back(y_one, rows, cols, v)
        ).astype(BF16)
    store_gin = pltpu.make_async_copy(gin_v, gin_hbm.at[0, 0], store_sem.at[1])
    store_gin.start()

    def summed(buf, count):
        total = buf[0]
        for s in range(1, count):
            total = total + buf[s]
        return total

    for copy in dp_copies:
        copy.wait_recv()
    buf_b[my_b] = summed(buf_a, n_dp)
    b_copies = [
        remote(buf_b.at[my_b], buf_b.at[my_b], b_ssem.at[s], b_rsem.at[s], {"space": dev})
        for s, dev in enumerate(peers_b)
    ]
    for copy in b_copies:
        copy.start()
    for copy in b_copies:
        copy.wait_recv()
    buf_c[my_c] = summed(buf_b, n_b)
    c_copies = [
        remote(buf_c.at[my_c], buf_c.at[my_c], c_ssem.at[s], c_rsem.at[s], {"space": dev})
        for s, dev in enumerate(peers_c)
    ]
    for copy in c_copies:
        copy.start()
    for copy in c_copies:
        copy.wait_recv()
    total = summed(buf_c, n_c)

    for main, shift, gw_ref, gb_ref in ((0, 0, gw1_ref, gb1_ref), (1, 32, gw2_ref, gb2_ref)):
        full = jnp.concatenate([total[main], roll(total[2], -shift)], axis=1)
        for a in range(3):
            part = full[a * rows_pad : a * rows_pad + rows_dev]
            for b in range(3):
                gw_ref[3 * a + b] = part[:, b * CH : (b + 1) * CH]
        bias_col = full[rows_pad : rows_pad + rows_dev, K3 : K3 + 1]
        eye_r = lax.broadcasted_iota(jnp.int32, (rows_dev, rows_dev), 0)
        eye_c = lax.broadcasted_iota(jnp.int32, (rows_dev, rows_dev), 1)
        spread = jnp.broadcast_to(bias_col, (rows_dev, rows_dev))
        gb_ref[...] = jnp.sum(jnp.where(eye_r == eye_c, spread, 0.0), axis=0)

    for copy in in_fwd + two_adj + act_fwd + one_adj + dp_copies + b_copies + c_copies:
        copy.wait_send()
    store_out.wait()
    store_gin.wait()


def on_device(n_dp, n_space, *args):
    rows_dev = CH // n_dp
    rows_pad = (rows_dev + 7) // 8 * 8
    n_c = 4
    n_b = n_space // n_c
    share = (3, 3 * rows_pad, LANES)
    field = args[0].shape
    anywhere = pl.BlockSpec(memory_space=pl.ANY)
    vmem = pl.BlockSpec(memory_space=pltpu.VMEM)
    smem = pl.BlockSpec(memory_space=pltpu.SMEM)
    dma = pltpu.SemaphoreType.DMA
    return pl.pallas_call(
        functools.partial(block_kernel, n_dp, n_space),
        out_shape=(
            jax.ShapeDtypeStruct(field, BF16),
            jax.ShapeDtypeStruct(field, BF16),
            jax.ShapeDtypeStruct((9, rows_dev, CH), F32),
            jax.ShapeDtypeStruct((rows_dev,), F32),
            jax.ShapeDtypeStruct((9, rows_dev, CH), F32),
            jax.ShapeDtypeStruct((rows_dev,), F32),
        ),
        in_specs=[anywhere, anywhere, vmem, vmem, vmem, vmem, smem, smem],
        out_specs=(anywhere, anywhere, vmem, vmem, vmem, vmem),
        scratch_shapes=[
            pltpu.VMEM((CH, GROUPS * LANES), BF16),
            pltpu.VMEM((CH, GROUPS * LANES), BF16),
            pltpu.VMEM((CH, GROUPS * LANES), BF16),
            pltpu.VMEM((CH, GROUPS * LANES), BF16),
            pltpu.VMEM((CH, GROUPS * LANES), BF16),
            pltpu.VMEM((CH, GROUPS * LANES), BF16),
            pltpu.VMEM((CH, GROUPS * LANES), F32),
            pltpu.VMEM((K3 + 16, WIDE), BF16),
            pltpu.VMEM((K3 + 16, WIDE), BF16),
            pltpu.VMEM((K3, WIDE), BF16),
            pltpu.VMEM((K3, WIDE), BF16),
            pltpu.VMEM((K3, WIDE), F32),
            pltpu.VMEM((K3, WIDE), F32),
            pltpu.VMEM((K3, WIDE), F32),
            pltpu.VMEM((2, 4, CH, LANES), BF16),
            pltpu.VMEM((2, 4, CH, LANES), BF16),
            pltpu.VMEM((2, 4, CH, LANES), BF16),
            pltpu.VMEM((2, 4, CH, LANES), BF16),
            pltpu.VMEM((n_dp,) + share, F32),
            pltpu.VMEM((n_dp,) + share, F32),
            pltpu.VMEM((n_b,) + share, F32),
            pltpu.VMEM((n_c,) + share, F32),
            dma((2,)),
            dma((2,)),
            dma((16,)),
            dma((16,)),
            dma((max(n_dp - 1, 1),)),
            dma((max(n_dp - 1, 1),)),
            dma((max(n_b - 1, 1),)),
            dma((max(n_b - 1, 1),)),
            dma((n_c - 1,)),
            dma((n_c - 1,)),
        ],
        compiler_params=pltpu.CompilerParams(
            collective_id=0, has_side_effects=True, vmem_limit_bytes=40 << 20
        ),
        name="unet_block",
    )(*args)


def solution(mesh):
    tiled = P("dp", "space", None, None)
    return jax.shard_map(
        functools.partial(on_device, mesh.shape["dp"], mesh.shape["space"]),
        mesh=mesh,
        in_specs=(tiled, tiled, P(), P(), P(), P(), P(), P()),
        out_specs=(tiled, tiled, P(None, "dp", None), P("dp"), P(None, "dp", None), P("dp")),
        check_vma=False,
    )
```

time: 463 us -> 49.5 us (0.11)
  the two profiles are of different devices: /device:TPU:24 before, /device:TPU:1 now
where the time goes in v1:
time: 49.5 us; the launch traced here: 49.3 us
  Pallas kernels  39.6 us (80%)
  local copies, waits for them, and re-layouts  8.97 us (18%)
  between operations  0.66 us (1%)
    pallas_call x1, Pallas kernels, on_device(): pl.pallas_call(functools.partial(block_kernel, n_dp, n_space), out_shape=...  39.6 us
    unnamed x22, local copies, waits for them, and re-layouts  8.97 us

profile of v1, /device:TPU:1, one launch (start us, length us, event | category | flops | bytes accessed | tf_op | source)
XLA Modules:
  0.0 49.3 jit_solution(9612437314077099957)
XLA Ops:
  0.6 0.0 copy-start.6
  0.6 0.8 %copy.15.rule_ref = s32[32,4]{1,0:T(8,128)S(1)} copy(s32[32,4]{0,1:T(4,128)} %param.15) | data formatting | bytes 1024 | tf_op args[7]
  1.4 0.0 copy-done.6
  1.4 0.0 copy-start.4
  1.4 0.0 copy-start.5
  1.4 0.1 copy.14.nb_ref
  1.5 0.5 %copy-done.4 = f32[48]{0:T(128)S(1)} copy-done((f32[48]{0:T(128)S(1)}, f32[48]{0:T(128)}, u32[]{:S(2)}) %copy-start.4) | copy-done | bytes 216
  2.1 0.0 copy-done.5
  2.1 0.0 copy-start
  2.1 1.0 %copy-done = bf16[1,1,48,4096]{3,2,1,0:T(8,128)(2,1)S(1)} copy-done((bf16[1,1,48,4096]{3,2,1,0:T(8,128)(2,1)S(1)}, bf16[1,1,48,4096]{3,2,1,0:T(8,128)(2,1)}, u32[]{:S(2)}) %copy-start) | copy-done | bytes 393240
  3.1 0.0 copy-start.1
  3.1 1.0 %copy-done.1 = bf16[1,1,48,4096]{3,2,1,0:T(8,128)(2,1)S(1)} copy-done((bf16[1,1,48,4096]{3,2,1,0:T(8,128)(2,1)S(1)}, bf16[1,1,48,4096]{3,2,1,0:T(8,128)(2,1)}, u32[]{:S(2)}) %copy-start.1) | copy-done | bytes 393240
  4.1 0.0 copy-start.2
  4.1 0.9 %copy-done.2 = bf16[9,48,48]{2,1,0:T(8,128)(2,1)S(1)} copy-done((bf16[9,48,48]{2,1,0:T(8,128)(2,1)S(1)}, bf16[9,48,48]{2,1,0:T(8,128)(2,1)}, u32[]{:S(2)}) %copy-start.2) | copy-done | bytes 41496
  5.0 0.0 copy-start.3
  5.0 0.9 %copy-done.3 = bf16[9,48,48]{2,1,0:T(8,128)(2,1)S(1)} copy-done((bf16[9,48,48]{2,1,0:T(8,128)(2,1)S(1)}, bf16[9,48,48]{2,1,0:T(8,128)(2,1)}, u32[]{:S(2)}) %copy-start.3) | copy-done | bytes 41496
  5.9 39.6 %unet_block.1 = (bf16[1,1,48,4096]{3,2,1,0:T(8,128)(2,1)S(1)}, bf16[1,1,48,4096]{3,2,1,0:T(8,128)(2,1)S(1)}, f32[9,6,48]{2,1,0:T(8,128)S(1)}, f32[6]{0:T(128)S(1...) custom-call(bf16[1,1,48,4096]{3,2,1,0:T(8,128)(2,1)S(1)} %copy-done, bf16[1,1,48,4096]{3,2,1,0:T(8,128)(2,1)S(1)} %copy-done.1, ...), custom_call_target="tpu_custom_call" | custom-call | tf_op jit(solution)/shard_map/unet_block/pallas_call | solution.py:468
  45.5 0.7 %copy.22 = bf16[1,1,48,4096]{3,2,1,0:T(8,128)(2,1)} copy(bf16[1,1,48,4096]{3,2,1,0:T(8,128)(2,1)S(1)} %get-tuple-element.12) | data formatting | bytes 786432
  46.3 0.7 %copy.23 = bf16[1,1,48,4096]{3,2,1,0:T(8,128)(2,1)} copy(bf16[1,1,48,4096]{3,2,1,0:T(8,128)(2,1)S(1)} %get-tuple-element.13) | data formatting | bytes 786432
  47.0 0.6 %copy.24 = f32[9,6,48]{2,1,0:T(8,128)} copy(f32[9,6,48]{2,1,0:T(8,128)S(1)} %get-tuple-element.14) | data formatting | bytes 20736
  47.6 0.5 %copy.25 = f32[6]{0:T(128)} copy(f32[6]{0:T(128)S(1)} %get-tuple-element.15) | data formatting | bytes 48
  48.2 0.6 %copy.26 = f32[9,6,48]{2,1,0:T(8,128)} copy(f32[9,6,48]{2,1,0:T(8,128)S(1)} %get-tuple-element.16) | data formatting | bytes 20736
  48.8 0.5 %copy.27 = f32[6]{0:T(128)} copy(f32[6]{0:T(128)S(1)} %get-tuple-element.17) | data formatting | bytes 48
Async XLA Ops:
  0.6 0.8 %copy-start.6 = (s32[32,4,3]{0,1,2:T(4,128)S(1)}, s32[32,4,3]{0,1,2:T(4,128)}, u32[]{:S(2)}) copy-start(s32[32,4,3]{0,1,2:T(4,128)} %param.14) | copy-start | bytes 4612
  1.4 0.7 %copy-start.4 = (f32[48]{0:T(128)S(1)}, f32[48]{0:T(128)}, u32[]{:S(2)}) copy-start(f32[48]{0:T(128)} %b1_ref.1) | copy-start | bytes 580
  1.4 0.7 %copy-start.5 = (f32[48]{0:T(128)S(1)}, f32[48]{0:T(128)}, u32[]{:S(2)}) copy-start(f32[48]{0:T(128)} %b2_ref.1) | copy-start | bytes 580
  2.1 1.0 %copy-start = (bf16[1,1,48,4096]{3,2,1,0:T(8,128)(2,1)S(1)}, bf16[1,1,48,4096]{3,2,1,0:T(8,128)(2,1)}, u32[]{:S(2)}) copy-start(bf16[1,1,48,4096]{3,2,1,0:T(8,128)(2,1)} %x_hbm.1) | copy-start | bytes 1179652
  3.1 1.0 %copy-start.1 = (bf16[1,1,48,4096]{3,2,1,0:T(8,128)(2,1)S(1)}, bf16[1,1,48,4096]{3,2,1,0:T(8,128)(2,1)}, u32[]{:S(2)}) copy-start(bf16[1,1,48,4096]{3,2,1,0:T(8,128)(2,1)} %g_hbm.1) | copy-start | bytes 1179652
  4.1 0.9 %copy-start.2 = (bf16[9,48,48]{2,1,0:T(8,128)(2,1)S(1)}, bf16[9,48,48]{2,1,0:T(8,128)(2,1)}, u32[]{:S(2)}) copy-start(bf16[9,48,48]{2,1,0:T(8,128)(2,1)} %w1_ref.1) | copy-start | bytes 124420
  5.0 0.9 %copy-start.3 = (bf16[9,48,48]{2,1,0:T(8,128)(2,1)S(1)}, bf16[9,48,48]{2,1,0:T(8,128)(2,1)}, u32[]{:S(2)}) copy-start(bf16[9,48,48]{2,1,0:T(8,128)(2,1)} %w2_ref.1) | copy-start | bytes 124420

commit v2 on v1

v2 whole, which is shorter than its diff:
```python
import functools
import math

import jax
import jax.numpy as jnp
from jax import lax
from jax.experimental import pallas as pl
from jax.experimental.pallas import tpu as pltpu
from jax.sharding import PartitionSpec as P

MESH = pl.DeviceIdType.MESH
F32 = jnp.float32
BF16 = jnp.bfloat16
LANES = 128
CH = 48
SIDE = 64
GROUPS = 32
EXTRA = 32
WIDE = (GROUPS + 1) * LANES
K3 = 3 * CH
ROOT = math.sqrt(2.0 / math.pi)


def grp(v):
    return slice(v * LANES, (v + 1) * LANES)


def roll(values, shift):
    shift = shift % LANES
    return pltpu.roll(values, shift, 1) if shift else values


def dot(a, b, dims):
    return lax.dot_general(a, b, (dims, ((), ())), preferred_element_type=F32)


def line_lane(edge, q):
    odd = (q & 1) == 1
    col_left = jnp.where(odd, q + 63, q)
    col_right = jnp.where(odd, (q + 126) & 127, q + 63)
    return jnp.where(
        edge == 0, q, jnp.where(edge == 2, q + 64, jnp.where(edge == 3, col_left, col_right))
    )


def halo_index(edge, lane):
    if edge == 0:
        return jnp.where(lane >= 64, lane - 64, -1000)
    if edge == 2:
        return jnp.where(lane < 64, lane, -1000)
    even = (lane & 1) == 0
    if edge == 3:
        return jnp.where(even, jnp.where(lane < 64, lane, lane - 63), -1000)
    return jnp.where(even, -1000, jnp.where(lane == 127, 1, jnp.where(lane >= 63, lane - 63, lane + 2)))


def line_index(line, lane):
    even = (lane & 1) == 0
    row = jnp.where(line == 0, lane, lane - 64)
    row = jnp.where((row >= 0) & (row < 64), row, -1000)
    left = jnp.where(even, jnp.where(lane < 64, lane, lane - 63), -1000)
    right = jnp.where(
        even, -1000, jnp.where(lane == 127, 1, jnp.where(lane >= 63, lane - 63, lane + 2))
    )
    return jnp.where((line & 1) == 0, row, jnp.where(line == 3, left, right))


def shifted_mover(edge, line, rotation, shift, end_weight):
    lane = lax.broadcasted_iota(jnp.int32, (8, LANES), 1)
    p = line_index(line, lane)
    q = jnp.where((rotation == 1) | (rotation == 2), 63 - p, p)
    valid = p >= 0
    tap = q + 1 - shift
    source = jnp.where(valid & (tap >= 0) & (tap < 64), line_lane(edge, tap), -1)
    rows = lax.broadcasted_iota(jnp.int32, (LANES, LANES), 0)
    table = jnp.where(rows == jnp.broadcast_to(source[0:1], (LANES, LANES)), 1.0, 0.0)
    if shift != 1:
        end = 0 if shift == 0 else 63
        corner = jnp.where(valid & (q == end), line_lane(edge, q), -1)
        table = table + jnp.where(
            rows == jnp.broadcast_to(corner[0:1], (LANES, LANES)), end_weight, 0.0
        )
    return table.astype(BF16)


def mover(edge, line, rotation):
    lane = lax.broadcasted_iota(jnp.int32, (8, LANES), 1)
    q = halo_index(edge, lane)
    turned = jnp.where((rotation == 1) | (rotation == 2), 63 - q, q)
    source = jnp.where(q < 0, -1, line_lane(line, turned))
    rows = lax.broadcasted_iota(jnp.int32, (LANES, LANES), 0)
    return jnp.where(rows == jnp.broadcast_to(source[0:1], (LANES, LANES)), 1.0, 0.0).astype(BF16)


def column(vector):
    rows = lax.broadcasted_iota(jnp.int32, (CH, CH), 0)
    cols = lax.broadcasted_iota(jnp.int32, (CH, CH), 1)
    spread = jnp.broadcast_to(vector, (CH, CH))
    return jnp.sum(jnp.where(rows == cols, spread, 0.0), axis=1, keepdims=True)


def block_kernel(
    n_dp,
    n_space,
    x_hbm,
    g_hbm,
    w1_hbm,
    b1_hbm,
    w2_hbm,
    b2_hbm,
    nb_hbm,
    rule_hbm,
    out_hbm,
    gin_hbm,
    gw1_ref,
    gb1_ref,
    gw2_ref,
    gb2_ref,
    x_v,
    g_v,
    w1_ref,
    b1_ref,
    w2_ref,
    b2_ref,
    nb_ref,
    rule_ref,
    dpre_v,
    out_v,
    gin_v,
    ex_v,
    ea_v,
    gs2_v,
    gs1_v,
    y_fwd,
    y_two,
    y_one,
    fwd_send,
    fwd_recv,
    tap_send,
    tap_recv,
    adj_send,
    adj_recv,
    part,
    buf_core,
    sum_core,
    buf_y,
    sum_y,
    buf_z,
    buf_x,
    load_sem,
    store_sem,
    halo_ssem,
    halo_rsem,
    red_ssem,
    red_rsem,
):
    hop = n_space // 4
    n_y, n_x, n_z = n_dp // 2, 4, n_space // 4
    rows_dev = CH // n_dp
    rows_pad = (rows_dev + 7) // 8 * 8
    me = lax.axis_index("space")
    my_dp = lax.axis_index("dp")
    core = lax.rem(me, 2)
    my_x = lax.div(me, hop)
    my_y, z_lo = lax.div(my_dp, 2), lax.rem(my_dp, 2)
    my_z = lax.div(lax.rem(me, hop), 2) * 2 + z_lo
    offsets = (-1, hop, 1, -hop)
    toward = [lax.rem(me + off + n_space, n_space) for off in offsets]
    reader = [lax.rem(me - off + n_space, n_space) for off in offsets]

    loads = [
        pltpu.make_async_copy(src, dst, load_sem.at[i])
        for i, (src, dst) in enumerate(
            (
                (nb_hbm, nb_ref),
                (rule_hbm, rule_ref),
                (x_hbm.at[0, 0], x_v),
                (g_hbm.at[0, 0], g_v),
                (w1_hbm, w1_ref),
                (w2_hbm, w2_ref),
                (b1_hbm, b1_ref),
                (b2_hbm, b2_ref),
            )
        )
    ]
    load_nb, load_rule, load_x, load_g, load_w1, load_w2, load_b1, load_b2 = loads

    core_peer = {"space": me + 1 - 2 * core}
    y_at = [lax.rem(my_y + s, n_y) for s in range(1, n_y)]
    y_peers = [{"dp": y * 2 + z_lo} for y in y_at]
    z_at = [lax.rem(my_z + s, n_z) for s in range(1, n_z)]
    z_peers = [
        {
            "dp": my_y * 2 + lax.rem(z, 2),
            "space": my_x * hop + lax.div(z, 2) * 2 + core,
        }
        for z in z_at
    ]
    in_x = lax.rem(me, hop)
    x_peers = [
        {"space": lax.rem(my_x + s, n_x) * hop + in_x + other * (1 - 2 * core)}
        for s in range(n_x)
        for other in range(2)
        if s or other
    ]

    barrier = pltpu.get_barrier_semaphore()
    everyone = [{"space": dev} for dev in toward] + [core_peer] + y_peers + z_peers + x_peers
    for dev in everyone:
        pl.semaphore_signal(barrier, inc=1, device_id=dev, device_id_type=MESH)
    for copy in loads:
        copy.start()

    lane = lax.broadcasted_iota(jnp.int32, (CH, LANES), 1)
    low = lane < 64
    first_col = (lane & 63) == 0
    last_col = (lane & 63) == 63
    edge_col = first_col | last_col
    zero = jnp.zeros((CH, LANES), F32)

    def remote(src, dst, ssem, rsem, device):
        return pltpu.make_async_remote_copy(
            src_ref=src,
            dst_ref=dst,
            send_sem=ssem,
            recv_sem=rsem,
            device_id=device,
            device_id_type=MESH,
        )

    def halo_copy(sends, recvs, slot, edge, dev):
        at = slot * 4 + edge
        return remote(
            sends.at[edge], recvs.at[edge], halo_ssem.at[at], halo_rsem.at[at], {"space": dev}
        )

    load_nb.wait()
    load_rule.wait()
    fwd_line = [nb_ref[1, e, reader[e]] for e in range(4)]
    fwd_turn = [nb_ref[2, e, reader[e]] for e in range(4)]
    own_line = [nb_ref[1, e, me] for e in range(4)]
    own_turn = [nb_ref[2, e, me] for e in range(4)]
    fwd_movers = [mover(e, fwd_line[e], fwd_turn[e]) for e in range(4)]

    def lines_of(group_of):
        rows = jnp.where(low, group_of(0), group_of(GROUPS - 1))
        cols = [zero, zero, zero, zero]
        for v in range(GROUPS):
            cols[v % 4] = cols[v % 4] + roll(jnp.where(edge_col, group_of(v), 0.0), 2 * v)
        cols = (cols[0] + cols[1]) + (cols[2] + cols[3])
        return rows.astype(BF16), cols.astype(BF16)

    def line_of(lines, edge):
        return jnp.where((fwd_line[edge] & 1) == 1, lines[1], lines[0])

    def forward_messages(lines, sends):
        for e in range(4):
            sends[e] = dot(line_of(lines, e), fwd_movers[e], ((1,), (0,))).astype(BF16)

    rules = [rule_ref[c, me] for c in range(4)]
    rule_at = jnp.where(
        lane == 64,
        rules[0],
        jnp.where(lane == 127, rules[1], jnp.where(lane == 0, rules[2], rules[3])),
    )
    first_weight = jnp.where(rule_at == 0, 1.0, jnp.where(rule_at == 1, 0.0, 0.5))
    corner_first = [jnp.where(r == 0, 1.0, jnp.where(r == 1, 0.0, 0.5)) for r in rules]
    end_weights = (
        (corner_first[0], corner_first[1]),
        (1.0 - corner_first[1], 1.0 - corner_first[3]),
        (corner_first[2], corner_first[3]),
        (1.0 - corner_first[0], 1.0 - corner_first[2]),
    )

    def tap_messages(lines, sends):
        for e in range(4):
            for s in range(3):
                move = shifted_mover(
                    e, own_line[e], own_turn[e], s, end_weights[e][0 if s == 0 else 1]
                )
                sends[e, s * CH : (s + 1) * CH, :] = dot(
                    lines[e % 2], move, ((1,), (0,))
                ).astype(BF16)

    def fill_inner(padded, v, here):
        padded[0:CH, grp(v)] = jnp.where(first_col, 0.0, roll(here, 1)).astype(BF16)
        padded[CH : 2 * CH, grp(v)] = here.astype(BF16)
        padded[2 * CH : K3, grp(v)] = jnp.where(last_col, 0.0, roll(here, -1)).astype(BF16)

    def fill_halo(padded, recvs):
        spread = recvs[1].astype(F32) + recvs[3].astype(F32)
        outer = recvs[0].astype(F32) + recvs[2].astype(F32)
        second = jnp.where(low, roll(spread, 2), roll(spread, 64))
        mean = ((outer + second) * 0.5).astype(BF16).astype(F32)
        corners = jnp.where(rule_at == 0, outer, jnp.where(rule_at == 1, second, mean))
        fill_inner(padded, EXTRA, outer)
        for v in range(GROUPS + 1):
            sides = (corners if v == EXTRA else roll(spread, -2 * v)).astype(BF16)
            padded[0:CH, grp(v)] = jnp.where(first_col, sides, padded[0:CH, grp(v)])
            padded[2 * CH : K3, grp(v)] = jnp.where(last_col, sides, padded[2 * CH : K3, grp(v)])

    def stacked(w_ref, tap_of):
        return jnp.concatenate(
            [
                jnp.concatenate([w_ref[tap_of(i, j)] for j in range(3)], axis=1)
                for i in range(3)
            ],
            axis=0,
        )

    def conv(weights, padded, y_ref):
        y_ref[...] = dot(weights, padded[0:K3, :], ((1,), (0,)))

    def conv_group(y_ref, v):
        prev = EXTRA if v == 0 else v - 1
        both = jnp.where(
            low,
            y_ref[0:CH, grp(v)] + y_ref[2 * CH : K3, grp(v + 1)],
            y_ref[2 * CH : K3, grp(v)] + y_ref[0:CH, grp(prev)],
        )
        return y_ref[CH : 2 * CH, grp(v)] + roll(both, 64)

    def stack_rows(grad_v, gs_ref):
        turned = None
        for v in range(GROUPS + 1):
            before = turned
            if v == EXTRA:
                gs_ref[CH : 2 * CH, grp(v)] = zero.astype(BF16)
                gs_ref[2 * CH : K3, grp(v)] = jnp.where(low, before, 0.0).astype(BF16)
                gs_ref[0:CH, grp(v - 1)] = jnp.where(low, before, 0.0).astype(BF16)
                gs_ref[0:CH, grp(v)] = jnp.where(
                    low, 0.0, roll(grad_v[:, grp(0)].astype(F32), 64)
                ).astype(BF16)
                continue
            here = grad_v[:, grp(v)]
            turned = roll(here.astype(F32), 64)
            gs_ref[CH : 2 * CH, grp(v)] = here
            gs_ref[2 * CH : K3, grp(v)] = jnp.where(
                low, 0.0 if v == 0 else before, turned
            ).astype(BF16)
            if v > 0:
                gs_ref[0:CH, grp(v - 1)] = jnp.where(low, before, turned).astype(BF16)

    def transpose_conv(weights, gs_ref, y_ref):
        y_ref[...] = dot(weights, gs_ref[...], ((0,), (0,)))

    def inner_group(y_ref, v):
        left = jnp.where(last_col, 0.0, roll(y_ref[0:CH, grp(v)], -1))
        right = jnp.where(first_col, 0.0, roll(y_ref[2 * CH : K3, grp(v)], 1))
        return y_ref[CH : 2 * CH, grp(v)] + (left + right)

    def adjoint_messages(y_ref, sends):
        def sides(v):
            return jnp.where(
                edge_col,
                jnp.where(last_col, y_ref[2 * CH : K3, grp(v)], y_ref[0:CH, grp(v)]),
                0.0,
            )

        cols = [zero, zero, zero, zero]
        for v in range(GROUPS):
            cols[v % 4] = cols[v % 4] + roll(sides(v), 2 * v)
        corners = sides(EXTRA)
        firsts = first_weight * corners
        seconds = corners - firsts
        cols = (
            (cols[0] + cols[1])
            + (cols[2] + cols[3])
            + roll(jnp.where(low, seconds, 0.0), -2)
            + roll(jnp.where(low, 0.0, seconds), 64)
        ).astype(BF16)
        rows = (inner_group(y_ref, EXTRA) + firsts).astype(BF16)
        for e in range(4):
            move = mover(e, own_line[e], own_turn[e])
            source = cols if e % 2 else rows
            sends[e] = dot(source, move, ((1,), (1,))).astype(BF16)

    def returned_lines(messages):
        rows, cols = zero, zero
        for e in range(4):
            is_col = (fwd_line[e] & 1) == 1
            rows = rows + jnp.where(is_col, 0.0, messages[e])
            cols = cols + jnp.where(is_col, messages[e], 0.0)
        return rows, cols

    def pulled_back(y_ref, rows, cols, v):
        total = inner_group(y_ref, v) + jnp.where(edge_col, roll(cols, -2 * v), 0.0)
        if v == 0:
            total = total + jnp.where(low, rows, 0.0)
        if v == GROUPS - 1:
            total = total + jnp.where(low, 0.0, rows)
        return total

    def put_part(grads, which):
        for d in range(n_dp):
            for a in range(3):
                at = a * CH + d * rows_dev
                to = a * rows_pad
                part[which, d, to : to + rows_dev, :] = grads[at : at + rows_dev, 0:LANES]
                part[
                    which, d, 3 * rows_pad : 3 * rows_pad + rows_dev, a * 32 : a * 32 + 32
                ] = grads[at : at + rows_dev, LANES : LANES + 32]

    def x_group(v):
        return x_v[:, grp(v)].astype(F32)

    def g_group(v):
        return g_v[:, grp(v)].astype(F32)

    def act_group(v):
        return ea_v[CH : 2 * CH, grp(v)].astype(F32)

    load_x.wait()
    forward_messages(lines_of(x_group), fwd_send.at[0])
    load_g.wait()
    tap_messages(lines_of(g_group), tap_send)
    pl.semaphore_wait(barrier, len(everyone))
    in_fwd = [halo_copy(fwd_send.at[0], fwd_recv.at[0], 0, e, reader[e]) for e in range(4)]
    two_tap = [halo_copy(tap_send, tap_recv, 1, e, toward[e]) for e in range(4)]
    for copy in in_fwd + two_tap:
        copy.start()

    part[...] = jnp.zeros(part.shape, F32)
    ex_v[K3 : K3 + 16, :] = jnp.ones((16, WIDE), BF16)
    ea_v[K3 : K3 + 16, :] = jnp.ones((16, WIDE), BF16)
    for v in range(GROUPS):
        fill_inner(ex_v, v, x_group(v))
    stack_rows(g_v, gs2_v)
    for copy in (load_w1, load_w2, load_b1, load_b2):
        copy.wait()
    w_one = stacked(w1_ref, lambda i, j: 3 * i + j)
    w_two = stacked(w2_ref, lambda i, j: 3 * i + j)
    w_two_by_col = stacked(w2_ref, lambda i, j: 3 * j + i)
    bias_one = jnp.broadcast_to(column(b1_ref[...].reshape(1, CH)), (CH, LANES))
    bias_two = jnp.broadcast_to(column(b2_ref[...].reshape(1, CH)), (CH, LANES))
    transpose_conv(w_two, gs2_v, y_two)

    for copy in in_fwd:
        copy.wait_recv()
    fill_halo(ex_v, fwd_recv.at[0])
    conv(w_one, ex_v, y_fwd)
    for copy in two_tap:
        copy.wait_recv()
    edge_weights = (
        w_two_by_col[:, 0:CH],
        w_two[:, 2 * CH : K3],
        w_two_by_col[:, 2 * CH : K3],
        w_two[:, 0:CH],
    )
    rows, cols = returned_lines(
        [dot(edge_weights[e], tap_recv[e], ((0,), (0,))) for e in range(4)]
    )
    for v in range(GROUPS):
        pre = conv_group(y_fwd, v) + bias_one
        square = pre * pre
        th = jnp.tanh(ROOT * (pre + 0.044715 * (square * pre)))
        cdf = 0.5 * (1.0 + th)
        fill_inner(ea_v, v, (pre * cdf).astype(BF16).astype(F32))
        slope = cdf + (0.5 * pre) * (1.0 - th * th) * (ROOT * (1.0 + (3.0 * 0.044715) * square))
        dpre_v[:, grp(v)] = (pulled_back(y_two, rows, cols, v) * slope).astype(BF16)

    act_lines = lines_of(act_group)
    forward_messages(act_lines, fwd_send.at[1])
    act_fwd = [halo_copy(fwd_send.at[1], fwd_recv.at[1], 2, e, reader[e]) for e in range(4)]
    for copy in act_fwd:
        copy.start()

    inner = slice(0, GROUPS * LANES)
    by_edge = [dot(tap_recv[e], line_of(act_lines, e), ((1,), (1,))) for e in range(4)]
    tail = jnp.zeros((CH, CH), F32)

    def halo_blocks(i):
        blocks = [tail, tail, tail]
        if i != 1:
            blocks = [by_edge[i][b * CH : (b + 1) * CH] for b in range(3)]
        blocks[0] = blocks[0] + by_edge[3][i * CH : (i + 1) * CH]
        blocks[2] = blocks[2] + by_edge[1][i * CH : (i + 1) * CH]
        return jnp.concatenate(blocks + [jnp.zeros((CH, 16), F32)], axis=1)

    halo_two = jnp.concatenate([halo_blocks(i) for i in range(3)], axis=0)
    put_part(dot(gs2_v[:, inner], ea_v[:, inner], ((1,), (1,))) + halo_two, 1)
    stack_rows(dpre_v, gs1_v)
    put_part(dot(gs1_v[...], ex_v[...], ((1,), (1,))), 0)
    core_copy = remote(
        part.at[1 - core], buf_core, red_ssem.at[0], red_rsem.at[0], core_peer
    )
    core_copy.start()

    transpose_conv(w_one, gs1_v, y_one)
    adjoint_messages(y_one, adj_send)
    one_adj = [halo_copy(adj_send, adj_recv, 3, e, toward[e]) for e in range(4)]
    for copy in one_adj:
        copy.start()

    core_copy.wait_recv()
    for d in range(n_dp):
        sum_core[d] = part[core, d] + buf_core[d]
    y_copies = [
        remote(
            sum_core.at[pl.ds(y * 2, 2)],
            buf_y.at[my_y],
            red_ssem.at[1 + s],
            red_rsem.at[1 + s],
            y_peers[s],
        )
        for s, y in enumerate(y_at)
    ]
    for copy in y_copies:
        copy.start()
    buf_y[my_y] = sum_core[pl.ds(my_y * 2, 2)]

    for copy in act_fwd:
        copy.wait_recv()
    fill_halo(ea_v, fwd_recv.at[1])
    conv(w_two, ea_v, y_fwd)
    for v in range(GROUPS):
        out_v[:, grp(v)] = (x_group(v) + conv_group(y_fwd, v) + bias_two).astype(BF16)
    store_out = pltpu.make_async_copy(out_v, out_hbm.at[0, 0], store_sem.at[0])
    store_out.start()

    def summed(buf, count):
        total = buf[0]
        for s in range(1, count):
            total = total + buf[s]
        return total

    for copy in y_copies:
        copy.wait_recv()
    sum_y[...] = summed(buf_y, n_y)
    at = n_y
    z_copies = [
        remote(
            sum_y.at[lax.rem(z, 2)],
            buf_z.at[my_z],
            red_ssem.at[at + s],
            red_rsem.at[at + s],
            z_peers[s],
        )
        for s, z in enumerate(z_at)
    ]
    for copy in z_copies:
        copy.start()
    buf_z[my_z] = sum_y[z_lo]

    for copy in one_adj:
        copy.wait_recv()
    rows, cols = returned_lines([adj_recv[e].astype(F32) for e in range(4)])
    for v in range(GROUPS):
        gin_v[:, grp(v)] = (g_group(v) + pulled_back(y_one, rows, cols, v)).astype(BF16)
    store_gin = pltpu.make_async_copy(gin_v, gin_hbm.at[0, 0], store_sem.at[1])
    store_gin.start()

    for copy in z_copies:
        copy.wait_recv()
    buf_x[core, my_x] = summed(buf_z, n_z)
    at = n_y + n_z - 1
    x_copies = [
        remote(
            buf_x.at[core, my_x],
            buf_x.at[core, my_x],
            red_ssem.at[at + s],
            red_rsem.at[at + s],
            dev,
        )
        for s, dev in enumerate(x_peers)
    ]
    for copy in x_copies:
        copy.start()
    for copy in x_copies:
        copy.wait_recv()

    for which, gw_ref, gb_ref in ((0, gw1_ref, gb1_ref), (1, gw2_ref, gb2_ref)):
        total = summed(buf_x.at[which], n_x)
        for a in range(3):
            full = jnp.concatenate(
                [
                    total[a * rows_pad : a * rows_pad + rows_dev],
                    total[3 * rows_pad : 3 * rows_pad + rows_dev, a * 32 : a * 32 + 32],
                ],
                axis=1,
            )
            for b in range(3):
                gw_ref[3 * a + b] = full[:, b * CH : (b + 1) * CH]
            if a == 1:
                eye_r = lax.broadcasted_iota(jnp.int32, (rows_dev, rows_dev), 0)
                eye_c = lax.broadcasted_iota(jnp.int32, (rows_dev, rows_dev), 1)
                spread = jnp.broadcast_to(full[:, K3 : K3 + 1], (rows_dev, rows_dev))
                gb_ref[...] = jnp.sum(jnp.where(eye_r == eye_c, spread, 0.0), axis=0)

    for copy in in_fwd + two_tap + act_fwd + one_adj + [core_copy]:
        copy.wait_send()
    for copy in y_copies + z_copies + x_copies:
        copy.wait_send()
    store_out.wait()
    store_gin.wait()


def write_kernel(count, *refs):
    sources, results, sem = refs[:count], refs[count : 2 * count], refs[2 * count]
    copies = [
        pltpu.make_async_copy(src, dst, sem.at[i])
        for i, (src, dst) in enumerate(zip(sources, results))
    ]
    for copy in copies:
        copy.start()
    for copy in copies:
        copy.wait()


def on_device(n_dp, n_space, x, g, w1, b1, w2, b2, neighbours, corner_rule):
    rows_dev = CH // n_dp
    rows_pad = (rows_dev + 7) // 8 * 8
    n_y, n_x, n_z = n_dp // 2, 4, n_space // 4
    share = (4 * rows_pad, LANES)
    field = x.shape
    shapes = (
        jax.ShapeDtypeStruct(field, BF16),
        jax.ShapeDtypeStruct(field, BF16),
        jax.ShapeDtypeStruct((9, rows_dev, CH), F32),
        jax.ShapeDtypeStruct((rows_dev,), F32),
        jax.ShapeDtypeStruct((9, rows_dev, CH), F32),
        jax.ShapeDtypeStruct((rows_dev,), F32),
    )
    anywhere = pl.BlockSpec(memory_space=pl.ANY)
    hbm = pl.BlockSpec(memory_space=pltpu.HBM)
    vmem = pl.BlockSpec(memory_space=pltpu.VMEM)
    dma = pltpu.SemaphoreType.DMA
    tile = (CH, GROUPS * LANES)
    reductions = 1 + (n_y - 1) + (n_z - 1) + (2 * n_x - 1)
    results = pl.pallas_call(
        functools.partial(block_kernel, n_dp, n_space),
        out_shape=shapes,
        in_specs=[hbm] * 8,
        out_specs=(anywhere, anywhere, vmem, vmem, vmem, vmem),
        scratch_shapes=[
            pltpu.VMEM(tile, BF16),
            pltpu.VMEM(tile, BF16),
            pltpu.VMEM((9, CH, CH), BF16),
            pltpu.VMEM((CH,), F32),
            pltpu.VMEM((9, CH, CH), BF16),
            pltpu.VMEM((CH,), F32),
            pltpu.SMEM((3, 4, n_space), jnp.int32),
            pltpu.SMEM((4, n_space), jnp.int32),
            pltpu.VMEM(tile, BF16),
            pltpu.VMEM(tile, BF16),
            pltpu.VMEM(tile, BF16),
            pltpu.VMEM((K3 + 16, WIDE), BF16),
            pltpu.VMEM((K3 + 16, WIDE), BF16),
            pltpu.VMEM((K3, WIDE), BF16),
            pltpu.VMEM((K3, WIDE), BF16),
            pltpu.VMEM((K3, WIDE), F32),
            pltpu.VMEM((K3, WIDE), F32),
            pltpu.VMEM((K3, WIDE), F32),
            pltpu.VMEM((2, 4, CH, LANES), BF16),
            pltpu.VMEM((2, 4, CH, LANES), BF16),
            pltpu.VMEM((4, K3, LANES), BF16),
            pltpu.VMEM((4, K3, LANES), BF16),
            pltpu.VMEM((4, CH, LANES), BF16),
            pltpu.VMEM((4, CH, LANES), BF16),
            pltpu.VMEM((2, n_dp) + share, F32),
            pltpu.VMEM((n_dp,) + share, F32),
            pltpu.VMEM((n_dp,) + share, F32),
            pltpu.VMEM((n_y, 2) + share, F32),
            pltpu.VMEM((2,) + share, F32),
            pltpu.VMEM((n_z,) + share, F32),
            pltpu.VMEM((2, n_x) + share, F32),
            dma((8,)),
            dma((2,)),
            dma((16,)),
            dma((16,)),
            dma((reductions,)),
            dma((reductions,)),
        ],
        compiler_params=pltpu.CompilerParams(
            collective_id=0, has_side_effects=True, vmem_limit_bytes=63 << 20
        ),
        name="unet_block",
    )(x, g, w1, b1, w2, b2, neighbours.transpose(2, 1, 0), corner_rule.T)
    return pl.pallas_call(
        functools.partial(write_kernel, len(shapes)),
        out_shape=shapes,
        in_specs=[anywhere] * len(shapes),
        out_specs=(hbm,) * len(shapes),
        scratch_shapes=[dma((len(shapes),))],
        name="write_results",
    )(*results)


def solution(mesh):
    tiled = P("dp", "space", None, None)
    return jax.shard_map(
        functools.partial(on_device, mesh.shape["dp"], mesh.shape["space"]),
        mesh=mesh,
        in_specs=(tiled, tiled, P(), P(), P(), P(), P(), P()),
        out_specs=(tiled, tiled, P(None, "dp", None), P("dp"), P(None, "dp", None), P("dp")),
        check_vma=False,
    )
```

time: 49.5 us -> 61.2 us (1.24)
  Pallas kernels: 39.6 us -> 60.5 us
  local copies, waits for them, and re-layouts: 8.97 us -> 0 us
    pallas_call x0 -> x1, Pallas kernels: none -> 26.7 us  [on_device(): pl.pallas_call(functools.partial(write_kernel, len(shapes)), out_shape=sh...]
    unnamed x22 -> x0, local copies, waits for them, and re-layouts: 8.97 us -> none
    pallas_call x1, Pallas kernels: 39.6 us -> 33.8 us  [on_device(): pl.pallas_call(functools.partial(block_kernel, n_dp, n_space), out_shape=...]
where the time goes in v2:
time: 61.2 us; the launch traced here: 61.1 us
  Pallas kernels  60.5 us (99%)
  between operations  0.64 us (1%)
    pallas_call x1, Pallas kernels, on_device(): pl.pallas_call(functools.partial(block_kernel, n_dp, n_space), out_shape=...  33.8 us
    pallas_call x1, Pallas kernels, on_device(): pl.pallas_call(functools.partial(write_kernel, len(shapes)), out_shape=sh...  26.7 us

profile of v2, /device:TPU:1, one launch (start us, length us, event | category | flops | bytes accessed | tf_op | source)
XLA Modules:
  0.0 61.1 jit_solution(18162493735229747521)
XLA Ops:
  0.6 33.8 %unet_block.1 = (bf16[1,1,48,4096]{3,2,1,0:T(8,128)(2,1)}, bf16[1,1,48,4096]{3,2,1,0:T(8,128)(2,1)}, f32[9,6,48]{2,1,0:T(8,128)}, f32[6]{0:T(128)}, f32[9,6,48]{2,1,0:T(8,128)}, /*index=5*/f32[6]{0:T(128)}) custom-call(bf16[1,1,48,4096]{3,2,1,0:T(8,128)(2,1)} %x_hbm.1, bf16[1,1,48,4096]{3,2,1,0:T(8,128)(2,1)} %g_hbm.1, bf16[9,48,48]{2,1,0:T(8,128)(2,1)} %w1_hbm.1, ...), custom_call_target="tpu_custom_call" | custom-call | tf_op jit(solution)/shard_map/unet_block/pallas_call | solution.py:630
  34.4 26.7 %write_results.1 = (bf16[1,1,48,4096]{3,2,1,0:T(8,128)(2,1)}, bf16[1,1,48,4096]{3,2,1,0:T(8,128)(2,1)}, f32[9,6,48]{2,1,0:T(8,128)}, f32[6]{0:T(128)}, f32[9,6,48]{2,1,0:T(8,128)}, /*index=5*/f32[6]{0:T(128)}) custom-call(bf16[1,1,48,4096]{3,2,1,0:T(8,128)(2,1)} %get-tuple-element.12.refs_0_, bf16[1,1,48,4096]{3,2,1,0:T(8,128)(2,1)} %get-tuple-element.13.refs_1_, ...), custom_call_target="tpu_custom_call" | custom-call | tf_op jit(solution)/shard_map/write_results/pallas_call | solution.py:679

commit v3 on v2

--- a/solution.py
+++ b/solution.py
@@ -110,8 +110,8 @@
     b2_hbm,
     nb_hbm,
     rule_hbm,
-    out_hbm,
-    gin_hbm,
+    out_ref,
+    gin_ref,
     gw1_ref,
     gb1_ref,
     gw2_ref,
@@ -125,8 +125,6 @@
     nb_ref,
     rule_ref,
     dpre_v,
-    out_v,
-    gin_v,
     ex_v,
     ea_v,
     gs2_v,
@@ -148,7 +146,6 @@
     buf_z,
     buf_x,
     load_sem,
-    store_sem,
     halo_ssem,
     halo_rsem,
     red_ssem,
@@ -514,9 +511,7 @@
     fill_halo(ea_v, fwd_recv.at[1])
     conv(w_two, ea_v, y_fwd)
     for v in range(GROUPS):
-        out_v[:, grp(v)] = (x_group(v) + conv_group(y_fwd, v) + bias_two).astype(BF16)
-    store_out = pltpu.make_async_copy(out_v, out_hbm.at[0, 0], store_sem.at[0])
-    store_out.start()
+        out_ref[0, 0, :, grp(v)] = (x_group(v) + conv_group(y_fwd, v) + bias_two).astype(BF16)
 
     def summed(buf, count):
         total = buf[0]
@@ -546,9 +541,7 @@
         copy.wait_recv()
     rows, cols = returned_lines([adj_recv[e].astype(F32) for e in range(4)])
     for v in range(GROUPS):
-        gin_v[:, grp(v)] = (g_group(v) + pulled_back(y_one, rows, cols, v)).astype(BF16)
-    store_gin = pltpu.make_async_copy(gin_v, gin_hbm.at[0, 0], store_sem.at[1])
-    store_gin.start()
+        gin_ref[0, 0, :, grp(v)] = (g_group(v) + pulled_back(y_one, rows, cols, v)).astype(BF16)
 
     for copy in z_copies:
         copy.wait_recv()
@@ -591,8 +584,6 @@
         copy.wait_send()
     for copy in y_copies + z_copies + x_copies:
         copy.wait_send()
-    store_out.wait()
-    store_gin.wait()
 
 
 def write_kernel(count, *refs):
@@ -621,17 +612,20 @@
         jax.ShapeDtypeStruct((9, rows_dev, CH), F32),
         jax.ShapeDtypeStruct((rows_dev,), F32),
     )
-    anywhere = pl.BlockSpec(memory_space=pl.ANY)
     hbm = pl.BlockSpec(memory_space=pltpu.HBM)
     vmem = pl.BlockSpec(memory_space=pltpu.VMEM)
     dma = pltpu.SemaphoreType.DMA
     tile = (CH, GROUPS * LANES)
     reductions = 1 + (n_y - 1) + (n_z - 1) + (2 * n_x - 1)
+    operands = [
+        pltpu.with_memory_space_constraint(leaf, pltpu.HBM)
+        for leaf in (x, g, w1, b1, w2, b2, neighbours.transpose(2, 1, 0), corner_rule.T)
+    ]
     results = pl.pallas_call(
         functools.partial(block_kernel, n_dp, n_space),
-        out_shape=shapes,
+        out_shape=tuple(pltpu.VMEM(leaf.shape, leaf.dtype) for leaf in shapes),
         in_specs=[hbm] * 8,
-        out_specs=(anywhere, anywhere, vmem, vmem, vmem, vmem),
+        out_specs=(vmem,) * len(shapes),
         scratch_shapes=[
             pltpu.VMEM(tile, BF16),
             pltpu.VMEM(tile, BF16),
@@ -641,8 +635,6 @@
             pltpu.VMEM((CH,), F32),
             pltpu.SMEM((3, 4, n_space), jnp.int32),
             pltpu.SMEM((4, n_space), jnp.int32),
-            pltpu.VMEM(tile, BF16),
-            pltpu.VMEM(tile, BF16),
             pltpu.VMEM(tile, BF16),
             pltpu.VMEM((K3 + 16, WIDE), BF16),
             pltpu.VMEM((K3 + 16, WIDE), BF16),
@@ -665,25 +657,24 @@
             pltpu.VMEM((n_z,) + share, F32),
             pltpu.VMEM((2, n_x) + share, F32),
             dma((8,)),
-            dma((2,)),
             dma((16,)),
             dma((16,)),
             dma((reductions,)),
             dma((reductions,)),
         ],
         compiler_params=pltpu.CompilerParams(
-            collective_id=0, has_side_effects=True, vmem_limit_bytes=63 << 20
+            collective_id=0, has_side_effects=True, vmem_limit_bytes=40 << 20
         ),
         name="unet_block",
-    )(x, g, w1, b1, w2, b2, neighbours.transpose(2, 1, 0), corner_rule.T)
+    )(*operands)
     return pl.pallas_call(
         functools.partial(write_kernel, len(shapes)),
         out_shape=shapes,
-        in_specs=[anywhere] * len(shapes),
+        in_specs=[vmem] * len(shapes),
         out_specs=(hbm,) * len(shapes),
         scratch_shapes=[dma((len(shapes),))],
         name="write_results",
-    )(*results)
+    )(*(pltpu.with_memory_space_constraint(leaf, pltpu.VMEM) for leaf in results))
 
 
 def solution(mesh):

time: 61.2 us -> 34.8 us (0.57)
  Pallas kernels: 60.5 us -> 34.1 us
    pallas_call x1, Pallas kernels: 26.7 us -> 0.94 us  [on_device(): pl.pallas_call(functools.partial(write_kernel, len(shapes)), out_shape=sh...]
    pallas_call x1, Pallas kernels: 33.8 us -> 33.1 us  [on_device(): pl.pallas_call(functools.partial(block_kernel, n_dp, n_space), out_shape=...]
where the time goes in v3:
time: 34.8 us; the launch traced here: 34.7 us
  Pallas kernels  34.1 us (98%)
  between operations  0.64 us (2%)
    pallas_call x1, Pallas kernels, on_device(): pl.pallas_call(functools.partial(block_kernel, n_dp, n_space), out_shape=...  33.1 us
    pallas_call x1, Pallas kernels, on_device(): pl.pallas_call(functools.partial(write_kernel, len(shapes)), out_shape=sh...  0.94 us

profile of v3, /device:TPU:1, one launch (start us, length us, event | category | flops | bytes accessed | tf_op | source)
XLA Modules:
  0.0 34.7 jit_solution(13094880238148707219)
XLA Ops:
  0.6 33.1 %unet_block.1 = (bf16[1,1,48,4096]{3,2,1,0:T(8,128)(2,1)S(1)}, bf16[1,1,48,4096]{3,2,1,0:T(8,128)(2,1)S(1)}, f32[9,6,48]{2,1,0:T(8,128)S(1)}, f32[6]{0:T(128)S(1...) custom-call(bf16[1,1,48,4096]{3,2,1,0:T(8,128)(2,1)} %x_hbm.1, bf16[1,1,48,4096]{3,2,1,0:T(8,128)(2,1)} %g_hbm.1, ...), custom_call_target="tpu_custom_call" | custom-call | tf_op jit(solution)/shard_map/unet_block/pallas_call | solution.py:624
  33.8 0.9 %write_results.1 = (bf16[1,1,48,4096]{3,2,1,0:T(8,128)(2,1)}, bf16[1,1,48,4096]{3,2,1,0:T(8,128)(2,1)}, f32[9,6,48]{2,1,0:T(8,128)}, f32[6]{0:T(128)}, f32[9,6,48]{2,1,0:T(8,128)}, /*index=5*/f32[6]{0:T(128)}) custom-call(bf16[1,1,48,4096]{3,2,1,0:T(8,128)(2,1)S(1)} %get-tuple-element.12.refs_0_, bf16[1,1,48,4096]{3,2,1,0:T(8,128)(2,1)S(1)} %get-tuple-element.13.refs_1_, ...), custom_call_target="tpu_custom_call" | custom-call | tf_op jit(solution)/shard_map/write_results/pallas_call | solution.py:670

commit v4 on v3

--- a/solution.py
+++ b/solution.py
@@ -239,13 +239,15 @@
     own_turn = [nb_ref[2, e, me] for e in range(4)]
     fwd_movers = [mover(e, fwd_line[e], fwd_turn[e]) for e in range(4)]
 
+    def collected(values_of):
+        cols = [zero, zero, zero, zero]
+        for v in range(GROUPS):
+            cols[v % 4] = cols[v % 4] + roll(jnp.where(edge_col, values_of(v), 0.0), 2 * v)
+        return (cols[0] + cols[1]) + (cols[2] + cols[3])
+
     def lines_of(group_of):
         rows = jnp.where(low, group_of(0), group_of(GROUPS - 1))
-        cols = [zero, zero, zero, zero]
-        for v in range(GROUPS):
-            cols[v % 4] = cols[v % 4] + roll(jnp.where(edge_col, group_of(v), 0.0), 2 * v)
-        cols = (cols[0] + cols[1]) + (cols[2] + cols[3])
-        return rows.astype(BF16), cols.astype(BF16)
+        return rows.astype(BF16), collected(group_of).astype(BF16)
 
     def line_of(lines, edge):
         return jnp.where((fwd_line[edge] & 1) == 1, lines[1], lines[0])
@@ -284,17 +286,24 @@
         padded[CH : 2 * CH, grp(v)] = here.astype(BF16)
         padded[2 * CH : K3, grp(v)] = jnp.where(last_col, 0.0, roll(here, -1)).astype(BF16)
 
-    def fill_halo(padded, recvs):
+    def fill_outer(padded, recvs):
         spread = recvs[1].astype(F32) + recvs[3].astype(F32)
         outer = recvs[0].astype(F32) + recvs[2].astype(F32)
         second = jnp.where(low, roll(spread, 2), roll(spread, 64))
         mean = ((outer + second) * 0.5).astype(BF16).astype(F32)
         corners = jnp.where(rule_at == 0, outer, jnp.where(rule_at == 1, second, mean))
         fill_inner(padded, EXTRA, outer)
-        for v in range(GROUPS + 1):
-            sides = (corners if v == EXTRA else roll(spread, -2 * v)).astype(BF16)
-            padded[0:CH, grp(v)] = jnp.where(first_col, sides, padded[0:CH, grp(v)])
-            padded[2 * CH : K3, grp(v)] = jnp.where(last_col, sides, padded[2 * CH : K3, grp(v)])
+        put_sides(padded, EXTRA, corners)
+        return spread
+
+    def put_sides(padded, v, sides):
+        sides = sides.astype(BF16)
+        padded[0:CH, grp(v)] = jnp.where(first_col, sides, padded[0:CH, grp(v)])
+        padded[2 * CH : K3, grp(v)] = jnp.where(last_col, sides, padded[2 * CH : K3, grp(v)])
+
+    def fill_columns(padded, spread):
+        for v in range(GROUPS):
+            put_sides(padded, v, roll(spread, -2 * v))
 
     def stacked(w_ref, tap_of):
         return jnp.concatenate(
@@ -305,16 +314,49 @@
             axis=0,
         )
 
+    odd_q = ((lane & 1) == 0) & (lane >= 64) | ((lane & 1) == 1) & ((lane < 63) | (lane == 127))
+
+    def with_corners(rows, cols):
+        to_rows = jnp.where(edge_col, jnp.where(low, cols, roll(cols, 66)), 0.0)
+        near = (lane == 0) | (lane == 63)
+        far = (lane == 126) | (lane == 61)
+        to_cols = jnp.where(near, rows, jnp.where(far, roll(rows, 62), 0.0))
+        return rows + to_rows, cols + to_cols
+
+    def halo_share(weights, padded, spread):
+        outer = dot(weights, padded[0:K3, grp(EXTRA)], ((1,), (0,)))
+        rows = roll(jnp.where(low, outer[2 * CH : K3], outer[0:CH]), 64)
+        left = dot(weights[:, 0:CH], spread, ((1,), (0,)))
+        right = dot(weights[:, 2 * CH : K3], spread, ((1,), (0,)))
+        even_lane = (lane & 1) == 0
+        taps = [
+            jnp.where(even_lane, left[a * CH : (a + 1) * CH], right[a * CH : (a + 1) * CH])
+            for a in range(3)
+        ]
+        onward = jnp.where(odd_q, roll(taps[0], 64), roll(taps[0], 66))
+        onward = jnp.where((lane == 0) | (lane == 63), 0.0, onward)
+        back = jnp.where(odd_q, roll(taps[2], 62), roll(taps[2], 64))
+        back = jnp.where((lane == 126) | (lane == 61), 0.0, back)
+        return with_corners(rows, taps[1] + (onward + back))
+
+    def gelu_and_slope(pre):
+        square = pre * pre
+        th = jnp.tanh(ROOT * (pre + 0.044715 * (square * pre)))
+        cdf = 0.5 * (1.0 + th)
+        slope = cdf + (0.5 * pre) * (1.0 - th * th) * (ROOT * (1.0 + (3.0 * 0.044715) * square))
+        return (pre * cdf).astype(BF16).astype(F32), slope
+
     def conv(weights, padded, y_ref):
         y_ref[...] = dot(weights, padded[0:K3, :], ((1,), (0,)))
 
-    def conv_group(y_ref, v):
+    def conv_group(y_ref, v, halo=True):
         prev = EXTRA if v == 0 else v - 1
-        both = jnp.where(
-            low,
-            y_ref[0:CH, grp(v)] + y_ref[2 * CH : K3, grp(v + 1)],
-            y_ref[2 * CH : K3, grp(v)] + y_ref[0:CH, grp(prev)],
-        )
+        above, below = y_ref[0:CH, grp(v)], y_ref[2 * CH : K3, grp(v)]
+        if halo or v < GROUPS - 1:
+            above = above + y_ref[2 * CH : K3, grp(v + 1)]
+        if halo or v > 0:
+            below = below + y_ref[0:CH, grp(prev)]
+        both = jnp.where(low, above, below)
         return y_ref[CH : 2 * CH, grp(v)] + roll(both, 64)
 
     def stack_rows(grad_v, gs_ref):
@@ -432,10 +474,31 @@
     bias_two = jnp.broadcast_to(column(b2_ref[...].reshape(1, CH)), (CH, LANES))
     transpose_conv(w_two, gs2_v, y_two)
 
+    inner = slice(0, GROUPS * LANES)
+    y_fwd[:, inner] = dot(w_one, ex_v[0:K3, inner], ((1,), (0,)))
+    pre_cols = [zero, zero, zero, zero]
+    back_cols = [zero, zero, zero, zero]
+    ends = {}
+    for v in range(GROUPS):
+        pre = conv_group(y_fwd, v, halo=False) + bias_one
+        back = inner_group(y_two, v)
+        pre_cols[v % 4] = pre_cols[v % 4] + roll(jnp.where(edge_col, pre, 0.0), 2 * v)
+        back_cols[v % 4] = back_cols[v % 4] + roll(jnp.where(edge_col, back, 0.0), 2 * v)
+        if v in (0, GROUPS - 1):
+            ends[v] = (pre, back)
+        act, slope = gelu_and_slope(pre)
+        fill_inner(ea_v, v, act)
+        dpre_v[:, grp(v)] = (back * slope).astype(BF16)
+    pre_rows, back_rows = [jnp.where(low, a, b) for a, b in zip(ends[0], ends[GROUPS - 1])]
+    pre_cols = (pre_cols[0] + pre_cols[1]) + (pre_cols[2] + pre_cols[3])
+    back_cols = (back_cols[0] + back_cols[1]) + (back_cols[2] + back_cols[3])
+
     for copy in in_fwd:
         copy.wait_recv()
-    fill_halo(ex_v, fwd_recv.at[0])
-    conv(w_one, ex_v, y_fwd)
+    in_spread = fill_outer(ex_v, fwd_recv.at[0])
+    more_rows, more_cols = halo_share(w_one, ex_v, in_spread.astype(BF16))
+    act_rows, slope_rows = gelu_and_slope(pre_rows + more_rows)
+    act_cols, slope_cols = gelu_and_slope(pre_cols + more_cols)
     for copy in two_tap:
         copy.wait_recv()
     edge_weights = (
@@ -444,25 +507,37 @@
         w_two_by_col[:, 2 * CH : K3],
         w_two[:, 0:CH],
     )
-    rows, cols = returned_lines(
-        [dot(edge_weights[e], tap_recv[e], ((0,), (0,))) for e in range(4)]
+    more_rows, more_cols = with_corners(
+        *returned_lines([dot(edge_weights[e], tap_recv[e], ((0,), (0,))) for e in range(4)])
     )
-    for v in range(GROUPS):
-        pre = conv_group(y_fwd, v) + bias_one
-        square = pre * pre
-        th = jnp.tanh(ROOT * (pre + 0.044715 * (square * pre)))
-        cdf = 0.5 * (1.0 + th)
-        fill_inner(ea_v, v, (pre * cdf).astype(BF16).astype(F32))
-        slope = cdf + (0.5 * pre) * (1.0 - th * th) * (ROOT * (1.0 + (3.0 * 0.044715) * square))
-        dpre_v[:, grp(v)] = (pulled_back(y_two, rows, cols, v) * slope).astype(BF16)
-
-    act_lines = lines_of(act_group)
+    dpre_rows = (back_rows + more_rows) * slope_rows
+    dpre_cols = (back_cols + more_cols) * slope_cols
+    act_lines = (act_rows.astype(BF16), act_cols.astype(BF16))
     forward_messages(act_lines, fwd_send.at[1])
     act_fwd = [halo_copy(fwd_send.at[1], fwd_recv.at[1], 2, e, reader[e]) for e in range(4)]
     for copy in act_fwd:
         copy.start()
 
-    inner = slice(0, GROUPS * LANES)
+    second_col, last_but_one = (lane & 63) == 1, (lane & 63) == 62
+    for v in range(GROUPS):
+        put = roll(act_cols, -2 * v)
+        row_half = low if v == 0 else jnp.logical_not(low)
+        back = jnp.where(edge_col, roll(dpre_cols, -2 * v).astype(BF16), dpre_v[:, grp(v)])
+        if v in (0, GROUPS - 1):
+            back = jnp.where(row_half, dpre_rows.astype(BF16), back)
+            here = jnp.where(edge_col, put, act_group(v))
+            fill_inner(ea_v, v, jnp.where(row_half, act_rows, here))
+        else:
+            for at, mask, values in (
+                (0, second_col, roll(put, 1)),
+                (CH, edge_col, put),
+                (2 * CH, last_but_one, roll(put, -1)),
+            ):
+                ea_v[at : at + CH, grp(v)] = jnp.where(
+                    mask, values.astype(BF16), ea_v[at : at + CH, grp(v)]
+                )
+        dpre_v[:, grp(v)] = back
+
     by_edge = [dot(tap_recv[e], line_of(act_lines, e), ((1,), (1,))) for e in range(4)]
     tail = jnp.zeros((CH, CH), F32)
 
@@ -477,10 +552,9 @@
     halo_two = jnp.concatenate([halo_blocks(i) for i in range(3)], axis=0)
     put_part(dot(gs2_v[:, inner], ea_v[:, inner], ((1,), (1,))) + halo_two, 1)
     stack_rows(dpre_v, gs1_v)
+    fill_columns(ex_v, in_spread)
     put_part(dot(gs1_v[...], ex_v[...], ((1,), (1,))), 0)
-    core_copy = remote(
-        part.at[1 - core], buf_core, red_ssem.at[0], red_rsem.at[0], core_peer
-    )
+    core_copy = remote(part.at[1 - core], buf_core, red_ssem.at[0], red_rsem.at[0], core_peer)
     core_copy.start()
 
     transpose_conv(w_one, gs1_v, y_one)
@@ -491,7 +565,7 @@
 
     core_copy.wait_recv()
     for d in range(n_dp):
-        sum_core[d] = part[core, d] + buf_core[d]
+        sum_core[d] = (part[core, d] + buf_core[d]).astype(BF16)
     y_copies = [
         remote(
             sum_core.at[pl.ds(y * 2, 2)],
@@ -508,20 +582,20 @@
 
     for copy in act_fwd:
         copy.wait_recv()
-    fill_halo(ea_v, fwd_recv.at[1])
+    fill_columns(ea_v, fill_outer(ea_v, fwd_recv.at[1]))
     conv(w_two, ea_v, y_fwd)
     for v in range(GROUPS):
         out_ref[0, 0, :, grp(v)] = (x_group(v) + conv_group(y_fwd, v) + bias_two).astype(BF16)
 
     def summed(buf, count):
-        total = buf[0]
+        total = buf[0].astype(F32)
         for s in range(1, count):
-            total = total + buf[s]
+            total = total + buf[s].astype(F32)
         return total
 
     for copy in y_copies:
         copy.wait_recv()
-    sum_y[...] = summed(buf_y, n_y)
+    sum_y[...] = summed(buf_y, n_y).astype(BF16)
     at = n_y
     z_copies = [
         remote(
@@ -651,10 +725,10 @@
             pltpu.VMEM((4, CH, LANES), BF16),
             pltpu.VMEM((2, n_dp) + share, F32),
             pltpu.VMEM((n_dp,) + share, F32),
-            pltpu.VMEM((n_dp,) + share, F32),
-            pltpu.VMEM((n_y, 2) + share, F32),
-            pltpu.VMEM((2,) + share, F32),
-            pltpu.VMEM((n_z,) + share, F32),
+            pltpu.VMEM((n_dp,) + share, BF16),
+            pltpu.VMEM((n_y, 2) + share, BF16),
+            pltpu.VMEM((2,) + share, BF16),
+            pltpu.VMEM((n_z,) + share, BF16),
             pltpu.VMEM((2, n_x) + share, F32),
             dma((8,)),
             dma((16,)),

time: 34.8 us -> 33.1 us (0.951)
  Pallas kernels: 34.1 us -> 32.3 us
    pallas_call x1, Pallas kernels: 33.1 us -> 31.4 us  [on_device(): pl.pallas_call(functools.partial(block_kernel, n_dp, n_space), out_shape=...]
where the time goes in v4:
time: 33.1 us; the launch traced here: 32.9 us
  Pallas kernels  32.3 us (98%)
  between operations  0.64 us (2%)
    pallas_call x1, Pallas kernels, on_device(): pl.pallas_call(functools.partial(block_kernel, n_dp, n_space), out_shape=...  31.4 us
    pallas_call x1, Pallas kernels, on_device(): pl.pallas_call(functools.partial(write_kernel, len(shapes)), out_shape=sh...  0.94 us

profile of v4, /device:TPU:1, one launch (start us, length us, event | category | flops | bytes accessed | tf_op | source)
XLA Modules:
  0.0 32.9 jit_solution(10883132109335841830)
XLA Ops:
  0.6 31.4 %unet_block.1 = (bf16[1,1,48,4096]{3,2,1,0:T(8,128)(2,1)S(1)}, bf16[1,1,48,4096]{3,2,1,0:T(8,128)(2,1)S(1)}, f32[9,6,48]{2,1,0:T(8,128)S(1)}, f32[6]{0:T(128)S(1...) custom-call(bf16[1,1,48,4096]{3,2,1,0:T(8,128)(2,1)} %x_hbm.1, bf16[1,1,48,4096]{3,2,1,0:T(8,128)(2,1)} %g_hbm.1, ...), custom_call_target="tpu_custom_call" | custom-call | tf_op jit(solution)/shard_map/unet_block/pallas_call | solution.py:698
  32.0 0.9 %write_results.1 = (bf16[1,1,48,4096]{3,2,1,0:T(8,128)(2,1)}, bf16[1,1,48,4096]{3,2,1,0:T(8,128)(2,1)}, f32[9,6,48]{2,1,0:T(8,128)}, f32[6]{0:T(128)}, f32[9,6,48]{2,1,0:T(8,128)}, /*index=5*/f32[6]{0:T(128)}) custom-call(bf16[1,1,48,4096]{3,2,1,0:T(8,128)(2,1)S(1)} %get-tuple-element.12.refs_0_, bf16[1,1,48,4096]{3,2,1,0:T(8,128)(2,1)S(1)} %get-tuple-element.13.refs_1_, ...), custom_call_target="tpu_custom_call" | custom-call | tf_op jit(solution)/shard_map/write_results/pallas_call | solution.py:744

commit v5 on v4

--- a/solution.py
+++ b/solution.py
@@ -124,6 +124,10 @@
     b2_ref,
     nb_ref,
     rule_ref,
+    act_first,
+    dpre_first,
+    pre_v,
+    back_v,
     dpre_v,
     ex_v,
     ea_v,
@@ -136,6 +140,7 @@
     fwd_recv,
     tap_send,
     tap_recv,
+    tap_move,
     adj_send,
     adj_recv,
     part,
@@ -150,6 +155,7 @@
     halo_rsem,
     red_ssem,
     red_rsem,
+    ready_sem,
 ):
     hop = n_space // 4
     n_y, n_x, n_z = n_dp // 2, 4, n_space // 4
@@ -202,8 +208,11 @@
     ]
 
     barrier = pltpu.get_barrier_semaphore()
-    everyone = [{"space": dev} for dev in toward] + [core_peer] + y_peers + z_peers + x_peers
-    for dev in everyone:
+    near = [{"space": dev} for dev in toward] + [core_peer]
+    near += [dev for s, dev in enumerate(y_peers, 1) if s in (1, n_y - 1)]
+    near += [dev for s, dev in enumerate(z_peers, 1) if s in (1, 2, n_z - 2, n_z - 1)]
+    near += [{"space": lax.rem(my_x + 2, n_x) * hop + in_x}]
+    for dev in near:
         pl.semaphore_signal(barrier, inc=1, device_id=dev, device_id_type=MESH)
     for copy in loads:
         copy.start()
@@ -214,6 +223,7 @@
     last_col = (lane & 63) == 63
     edge_col = first_col | last_col
     zero = jnp.zeros((CH, LANES), F32)
+    blank = jnp.zeros((CH, LANES), BF16)
 
     def remote(src, dst, ssem, rsem, device):
         return pltpu.make_async_remote_copy(
@@ -240,14 +250,16 @@
     fwd_movers = [mover(e, fwd_line[e], fwd_turn[e]) for e in range(4)]
 
     def collected(values_of):
-        cols = [zero, zero, zero, zero]
+        cols = [zero, zero]
         for v in range(GROUPS):
-            cols[v % 4] = cols[v % 4] + roll(jnp.where(edge_col, values_of(v), 0.0), 2 * v)
-        return (cols[0] + cols[1]) + (cols[2] + cols[3])
+            cols[v % 2] = cols[v % 2] + roll(jnp.where(edge_col, values_of(v), 0.0), 2 * v)
+        return cols[0] + cols[1]
 
     def lines_of(group_of):
-        rows = jnp.where(low, group_of(0), group_of(GROUPS - 1))
-        return rows.astype(BF16), collected(group_of).astype(BF16)
+        return [form.astype(BF16) for form in edges_of(group_of)]
+
+    def edges_of(group_of):
+        return jnp.where(low, group_of(0), group_of(GROUPS - 1)), collected(group_of)
 
     def line_of(lines, edge):
         return jnp.where((fwd_line[edge] & 1) == 1, lines[1], lines[0])
@@ -263,28 +275,31 @@
         jnp.where(lane == 127, rules[1], jnp.where(lane == 0, rules[2], rules[3])),
     )
     first_weight = jnp.where(rule_at == 0, 1.0, jnp.where(rule_at == 1, 0.0, 0.5))
-    corner_first = [jnp.where(r == 0, 1.0, jnp.where(r == 1, 0.0, 0.5)) for r in rules]
-    end_weights = (
-        (corner_first[0], corner_first[1]),
-        (1.0 - corner_first[1], 1.0 - corner_first[3]),
-        (corner_first[2], corner_first[3]),
-        (1.0 - corner_first[0], 1.0 - corner_first[2]),
-    )
-
-    def tap_messages(lines, sends):
+    def end_weights(edge):
+        ends = ((0, 1), (1, 3), (2, 3), (0, 2))[edge]
+        weights = []
+        for c in ends:
+            rule = rule_ref[c, reader[edge]]
+            first = jnp.where(rule == 0, 1.0, jnp.where(rule == 1, 0.0, 0.5))
+            weights.append(1.0 - first if edge % 2 else first)
+        return weights
+
+    def tap_movers(moves):
         for e in range(4):
+            first, last = end_weights(e)
             for s in range(3):
-                move = shifted_mover(
-                    e, own_line[e], own_turn[e], s, end_weights[e][0 if s == 0 else 1]
+                moves[e, :, s * LANES : (s + 1) * LANES] = shifted_mover(
+                    e, fwd_line[e], fwd_turn[e], s, first if s == 0 else last
                 )
-                sends[e, s * CH : (s + 1) * CH, :] = dot(
-                    lines[e % 2], move, ((1,), (0,))
-                ).astype(BF16)
+
+    def shifted_taps(lines, moves):
+        wide = dot(lines, moves, ((1,), (0,))).astype(BF16)
+        return jnp.concatenate([wide[:, s * LANES : (s + 1) * LANES] for s in range(3)], axis=0)
 
     def fill_inner(padded, v, here):
-        padded[0:CH, grp(v)] = jnp.where(first_col, 0.0, roll(here, 1)).astype(BF16)
-        padded[CH : 2 * CH, grp(v)] = here.astype(BF16)
-        padded[2 * CH : K3, grp(v)] = jnp.where(last_col, 0.0, roll(here, -1)).astype(BF16)
+        padded[0:CH, grp(v)] = jnp.where(first_col, blank, roll(here, 1))
+        padded[CH : 2 * CH, grp(v)] = here
+        padded[2 * CH : K3, grp(v)] = jnp.where(last_col, blank, roll(here, -1))
 
     def fill_outer(padded, recvs):
         spread = recvs[1].astype(F32) + recvs[3].astype(F32)
@@ -292,12 +307,11 @@
         second = jnp.where(low, roll(spread, 2), roll(spread, 64))
         mean = ((outer + second) * 0.5).astype(BF16).astype(F32)
         corners = jnp.where(rule_at == 0, outer, jnp.where(rule_at == 1, second, mean))
-        fill_inner(padded, EXTRA, outer)
-        put_sides(padded, EXTRA, corners)
-        return spread
+        fill_inner(padded, EXTRA, outer.astype(BF16))
+        put_sides(padded, EXTRA, corners.astype(BF16))
+        return spread.astype(BF16)
 
     def put_sides(padded, v, sides):
-        sides = sides.astype(BF16)
         padded[0:CH, grp(v)] = jnp.where(first_col, sides, padded[0:CH, grp(v)])
         padded[2 * CH : K3, grp(v)] = jnp.where(last_col, sides, padded[2 * CH : K3, grp(v)])
 
@@ -361,24 +375,17 @@
 
     def stack_rows(grad_v, gs_ref):
         turned = None
-        for v in range(GROUPS + 1):
-            before = turned
-            if v == EXTRA:
-                gs_ref[CH : 2 * CH, grp(v)] = zero.astype(BF16)
-                gs_ref[2 * CH : K3, grp(v)] = jnp.where(low, before, 0.0).astype(BF16)
-                gs_ref[0:CH, grp(v - 1)] = jnp.where(low, before, 0.0).astype(BF16)
-                gs_ref[0:CH, grp(v)] = jnp.where(
-                    low, 0.0, roll(grad_v[:, grp(0)].astype(F32), 64)
-                ).astype(BF16)
-                continue
-            here = grad_v[:, grp(v)]
-            turned = roll(here.astype(F32), 64)
+        for v in range(GROUPS):
+            before, here = turned, grad_v[:, grp(v)]
+            turned = roll(here, 64)
             gs_ref[CH : 2 * CH, grp(v)] = here
-            gs_ref[2 * CH : K3, grp(v)] = jnp.where(
-                low, 0.0 if v == 0 else before, turned
-            ).astype(BF16)
+            gs_ref[2 * CH : K3, grp(v)] = jnp.where(low, blank if v == 0 else before, turned)
             if v > 0:
-                gs_ref[0:CH, grp(v - 1)] = jnp.where(low, before, turned).astype(BF16)
+                gs_ref[0:CH, grp(v - 1)] = jnp.where(low, before, turned)
+        gs_ref[CH : 2 * CH, grp(EXTRA)] = blank
+        gs_ref[2 * CH : K3, grp(EXTRA)] = jnp.where(low, turned, blank)
+        gs_ref[0:CH, grp(EXTRA - 1)] = jnp.where(low, turned, blank)
+        gs_ref[0:CH, grp(EXTRA)] = jnp.where(low, blank, roll(grad_v[:, grp(0)], 64))
 
     def transpose_conv(weights, gs_ref, y_ref):
         y_ref[...] = dot(weights, gs_ref[...], ((0,), (0,)))
@@ -452,18 +459,30 @@
     load_x.wait()
     forward_messages(lines_of(x_group), fwd_send.at[0])
     load_g.wait()
-    tap_messages(lines_of(g_group), tap_send)
-    pl.semaphore_wait(barrier, len(everyone))
+    tap_send[0], tap_send[1] = lines_of(g_group)
+    pl.semaphore_wait(barrier, len(near))
     in_fwd = [halo_copy(fwd_send.at[0], fwd_recv.at[0], 0, e, reader[e]) for e in range(4)]
-    two_tap = [halo_copy(tap_send, tap_recv, 1, e, toward[e]) for e in range(4)]
+    two_tap = [
+        remote(
+            tap_send.at[e % 2],
+            tap_recv.at[e],
+            halo_ssem.at[4 + e],
+            halo_rsem.at[4 + e],
+            {"space": toward[e]},
+        )
+        for e in range(4)
+    ]
     for copy in in_fwd + two_tap:
         copy.start()
 
+    for dev in near:
+        pl.semaphore_signal(ready_sem, inc=1, device_id=dev, device_id_type=MESH)
+    tap_movers(tap_move)
     part[...] = jnp.zeros(part.shape, F32)
     ex_v[K3 : K3 + 16, :] = jnp.ones((16, WIDE), BF16)
     ea_v[K3 : K3 + 16, :] = jnp.ones((16, WIDE), BF16)
     for v in range(GROUPS):
-        fill_inner(ex_v, v, x_group(v))
+        fill_inner(ex_v, v, x_v[:, grp(v)])
     stack_rows(g_v, gs2_v)
     for copy in (load_w1, load_w2, load_b1, load_b2):
         copy.wait()
@@ -476,31 +495,24 @@
 
     inner = slice(0, GROUPS * LANES)
     y_fwd[:, inner] = dot(w_one, ex_v[0:K3, inner], ((1,), (0,)))
-    pre_cols = [zero, zero, zero, zero]
-    back_cols = [zero, zero, zero, zero]
-    ends = {}
     for v in range(GROUPS):
-        pre = conv_group(y_fwd, v, halo=False) + bias_one
-        back = inner_group(y_two, v)
-        pre_cols[v % 4] = pre_cols[v % 4] + roll(jnp.where(edge_col, pre, 0.0), 2 * v)
-        back_cols[v % 4] = back_cols[v % 4] + roll(jnp.where(edge_col, back, 0.0), 2 * v)
-        if v in (0, GROUPS - 1):
-            ends[v] = (pre, back)
-        act, slope = gelu_and_slope(pre)
-        fill_inner(ea_v, v, act)
-        dpre_v[:, grp(v)] = (back * slope).astype(BF16)
-    pre_rows, back_rows = [jnp.where(low, a, b) for a, b in zip(ends[0], ends[GROUPS - 1])]
-    pre_cols = (pre_cols[0] + pre_cols[1]) + (pre_cols[2] + pre_cols[3])
-    back_cols = (back_cols[0] + back_cols[1]) + (back_cols[2] + back_cols[3])
-
-    for copy in in_fwd:
+        pre_v[:, grp(v)] = conv_group(y_fwd, v, halo=False) + bias_one
+    for v in range(GROUPS):
+        back_v[:, grp(v)] = inner_group(y_two, v)
+    for v in range(GROUPS):
+        act, slope = gelu_and_slope(pre_v[:, grp(v)])
+        act_first[:, grp(v)] = act.astype(BF16)
+        dpre_first[:, grp(v)] = (back_v[:, grp(v)] * slope).astype(BF16)
+    pre_rows, pre_cols = edges_of(lambda v: pre_v[:, grp(v)])
+    back_rows, back_cols = edges_of(lambda v: back_v[:, grp(v)])
+
+    for copy in in_fwd + two_tap:
         copy.wait_recv()
     in_spread = fill_outer(ex_v, fwd_recv.at[0])
-    more_rows, more_cols = halo_share(w_one, ex_v, in_spread.astype(BF16))
+    more_rows, more_cols = halo_share(w_one, ex_v, in_spread)
     act_rows, slope_rows = gelu_and_slope(pre_rows + more_rows)
     act_cols, slope_cols = gelu_and_slope(pre_cols + more_cols)
-    for copy in two_tap:
-        copy.wait_recv()
+    taps = [shifted_taps(tap_recv[e], tap_move[e]) for e in range(4)]
     edge_weights = (
         w_two_by_col[:, 0:CH],
         w_two[:, 2 * CH : K3],
@@ -508,7 +520,7 @@
         w_two[:, 0:CH],
     )
     more_rows, more_cols = with_corners(
-        *returned_lines([dot(edge_weights[e], tap_recv[e], ((0,), (0,))) for e in range(4)])
+        *returned_lines([dot(edge_weights[e], taps[e], ((0,), (0,))) for e in range(4)])
     )
     dpre_rows = (back_rows + more_rows) * slope_rows
     dpre_cols = (back_cols + more_cols) * slope_cols
@@ -518,27 +530,18 @@
     for copy in act_fwd:
         copy.start()
 
-    second_col, last_but_one = (lane & 63) == 1, (lane & 63) == 62
+    back_lines = (dpre_rows.astype(BF16), dpre_cols.astype(BF16))
     for v in range(GROUPS):
-        put = roll(act_cols, -2 * v)
-        row_half = low if v == 0 else jnp.logical_not(low)
-        back = jnp.where(edge_col, roll(dpre_cols, -2 * v).astype(BF16), dpre_v[:, grp(v)])
+        here = jnp.where(edge_col, roll(act_lines[1], -2 * v), act_first[:, grp(v)])
+        back = jnp.where(edge_col, roll(back_lines[1], -2 * v), dpre_first[:, grp(v)])
         if v in (0, GROUPS - 1):
-            back = jnp.where(row_half, dpre_rows.astype(BF16), back)
-            here = jnp.where(edge_col, put, act_group(v))
-            fill_inner(ea_v, v, jnp.where(row_half, act_rows, here))
-        else:
-            for at, mask, values in (
-                (0, second_col, roll(put, 1)),
-                (CH, edge_col, put),
-                (2 * CH, last_but_one, roll(put, -1)),
-            ):
-                ea_v[at : at + CH, grp(v)] = jnp.where(
-                    mask, values.astype(BF16), ea_v[at : at + CH, grp(v)]
-                )
+            row_half = low if v == 0 else jnp.logical_not(low)
+            here = jnp.where(row_half, act_lines[0], here)
+            back = jnp.where(row_half, back_lines[0], back)
+        fill_inner(ea_v, v, here)
         dpre_v[:, grp(v)] = back
 
-    by_edge = [dot(tap_recv[e], line_of(act_lines, e), ((1,), (1,))) for e in range(4)]
+    by_edge = [dot(taps[e], line_of(act_lines, e), ((1,), (1,))) for e in range(4)]
     tail = jnp.zeros((CH, CH), F32)
 
     def halo_blocks(i):
@@ -576,6 +579,7 @@
         )
         for s, y in enumerate(y_at)
     ]
+    pl.semaphore_wait(ready_sem, len(near))
     for copy in y_copies:
         copy.start()
     buf_y[my_y] = sum_core[pl.ds(my_y * 2, 2)]
@@ -710,6 +714,10 @@
             pltpu.SMEM((3, 4, n_space), jnp.int32),
             pltpu.SMEM((4, n_space), jnp.int32),
             pltpu.VMEM(tile, BF16),
+            pltpu.VMEM(tile, BF16),
+            pltpu.VMEM(tile, F32),
+            pltpu.VMEM(tile, F32),
+            pltpu.VMEM(tile, BF16),
             pltpu.VMEM((K3 + 16, WIDE), BF16),
             pltpu.VMEM((K3 + 16, WIDE), BF16),
             pltpu.VMEM((K3, WIDE), BF16),
@@ -719,8 +727,9 @@
             pltpu.VMEM((K3, WIDE), F32),
             pltpu.VMEM((2, 4, CH, LANES), BF16),
             pltpu.VMEM((2, 4, CH, LANES), BF16),
-            pltpu.VMEM((4, K3, LANES), BF16),
-            pltpu.VMEM((4, K3, LANES), BF16),
+            pltpu.VMEM((2, CH, LANES), BF16),
+            pltpu.VMEM((4, CH, LANES), BF16),
+            pltpu.VMEM((4, LANES, 3 * LANES), BF16),
             pltpu.VMEM((4, CH, LANES), BF16),
             pltpu.VMEM((4, CH, LANES), BF16),
             pltpu.VMEM((2, n_dp) + share, F32),
@@ -735,6 +744,7 @@
             dma((16,)),
             dma((reductions,)),
             dma((reductions,)),
+            pltpu.SemaphoreType.REGULAR,
         ],
         compiler_params=pltpu.CompilerParams(
             collective_id=0, has_side_effects=True, vmem_limit_bytes=40 << 20

time: 33.1 us -> 32.6 us (0.985)
  Pallas kernels: 32.3 us -> 31.8 us
    pallas_call x1, Pallas kernels: 31.4 us -> 30.9 us  [on_device(): pl.pallas_call(functools.partial(block_kernel, n_dp, n_space), out_shape=...]
where the time goes in v5:
time: 32.6 us; the launch traced here: 32.5 us
  Pallas kernels  31.8 us (98%)
  between operations  0.64 us (2%)
    pallas_call x1, Pallas kernels, on_device(): pl.pallas_call(functools.partial(block_kernel, n_dp, n_space), out_shape=...  30.9 us
    pallas_call x1, Pallas kernels, on_device(): pl.pallas_call(functools.partial(write_kernel, len(shapes)), out_shape=sh...  0.94 us

profile of v5, /device:TPU:1, one launch (start us, length us, event | category | flops | bytes accessed | tf_op | source)
XLA Modules:
  0.0 32.5 jit_solution(11518573603960511868)
XLA Ops:
  0.6 30.9 %unet_block.1 = (bf16[1,1,48,4096]{3,2,1,0:T(8,128)(2,1)S(1)}, bf16[1,1,48,4096]{3,2,1,0:T(8,128)(2,1)S(1)}, f32[9,6,48]{2,1,0:T(8,128)S(1)}, f32[6]{0:T(128)S(1...) custom-call(bf16[1,1,48,4096]{3,2,1,0:T(8,128)(2,1)} %x_hbm.1, bf16[1,1,48,4096]{3,2,1,0:T(8,128)(2,1)} %g_hbm.1, ...), custom_call_target="tpu_custom_call" | custom-call | tf_op jit(solution)/shard_map/unet_block/pallas_call | solution.py:702
  31.5 0.9 %write_results.1 = (bf16[1,1,48,4096]{3,2,1,0:T(8,128)(2,1)}, bf16[1,1,48,4096]{3,2,1,0:T(8,128)(2,1)}, f32[9,6,48]{2,1,0:T(8,128)}, f32[6]{0:T(128)}, f32[9,6,48]{2,1,0:T(8,128)}, /*index=5*/f32[6]{0:T(128)}) custom-call(bf16[1,1,48,4096]{3,2,1,0:T(8,128)(2,1)S(1)} %get-tuple-element.12.refs_0_, bf16[1,1,48,4096]{3,2,1,0:T(8,128)(2,1)S(1)} %get-tuple-element.13.refs_1_, ...), custom_call_target="tpu_custom_call" | custom-call | tf_op jit(solution)/shard_map/write_results/pallas_call | solution.py:754

commit v6 on v5

--- a/solution.py
+++ b/solution.py
@@ -144,6 +144,8 @@
     adj_send,
     adj_recv,
     part,
+    part_out,
+    part_own,
     buf_core,
     sum_core,
     buf_y,
@@ -437,15 +439,15 @@
             total = total + jnp.where(low, 0.0, rows)
         return total
 
-    def put_part(grads, which):
+    def cut(grads):
         for d in range(n_dp):
             for a in range(3):
                 at = a * CH + d * rows_dev
                 to = a * rows_pad
-                part[which, d, to : to + rows_dev, :] = grads[at : at + rows_dev, 0:LANES]
-                part[
-                    which, d, 3 * rows_pad : 3 * rows_pad + rows_dev, a * 32 : a * 32 + 32
-                ] = grads[at : at + rows_dev, LANES : LANES + 32]
+                part[d, to : to + rows_dev, :] = grads[at : at + rows_dev, 0:LANES]
+                part[d, 3 * rows_pad : 3 * rows_pad + rows_dev, a * 32 : a * 32 + 32] = grads[
+                    at : at + rows_dev, LANES : LANES + 32
+                ]
 
     def x_group(v):
         return x_v[:, grp(v)].astype(F32)
@@ -479,6 +481,8 @@
         pl.semaphore_signal(ready_sem, inc=1, device_id=dev, device_id_type=MESH)
     tap_movers(tap_move)
     part[...] = jnp.zeros(part.shape, F32)
+    part_out[...] = jnp.zeros(part_out.shape, F32)
+    part_own[...] = jnp.zeros(part_own.shape, F32)
     ex_v[K3 : K3 + 16, :] = jnp.ones((16, WIDE), BF16)
     ea_v[K3 : K3 + 16, :] = jnp.ones((16, WIDE), BF16)
     for v in range(GROUPS):
@@ -525,50 +529,59 @@
     dpre_rows = (back_rows + more_rows) * slope_rows
     dpre_cols = (back_cols + more_cols) * slope_cols
     act_lines = (act_rows.astype(BF16), act_cols.astype(BF16))
-    forward_messages(act_lines, fwd_send.at[1])
-    act_fwd = [halo_copy(fwd_send.at[1], fwd_recv.at[1], 2, e, reader[e]) for e in range(4)]
-    for copy in act_fwd:
-        copy.start()
-
     back_lines = (dpre_rows.astype(BF16), dpre_cols.astype(BF16))
-    for v in range(GROUPS):
-        here = jnp.where(edge_col, roll(act_lines[1], -2 * v), act_first[:, grp(v)])
-        back = jnp.where(edge_col, roll(back_lines[1], -2 * v), dpre_first[:, grp(v)])
+
+    def patched(first, lines, v):
+        here = jnp.where(edge_col, roll(lines[1], -2 * v), first[:, grp(v)])
         if v in (0, GROUPS - 1):
-            row_half = low if v == 0 else jnp.logical_not(low)
-            here = jnp.where(row_half, act_lines[0], here)
-            back = jnp.where(row_half, back_lines[0], back)
-        fill_inner(ea_v, v, here)
-        dpre_v[:, grp(v)] = back
-
-    by_edge = [dot(taps[e], line_of(act_lines, e), ((1,), (1,))) for e in range(4)]
-    tail = jnp.zeros((CH, CH), F32)
-
-    def halo_blocks(i):
-        blocks = [tail, tail, tail]
-        if i != 1:
-            blocks = [by_edge[i][b * CH : (b + 1) * CH] for b in range(3)]
-        blocks[0] = blocks[0] + by_edge[3][i * CH : (i + 1) * CH]
-        blocks[2] = blocks[2] + by_edge[1][i * CH : (i + 1) * CH]
-        return jnp.concatenate(blocks + [jnp.zeros((CH, 16), F32)], axis=1)
-
-    halo_two = jnp.concatenate([halo_blocks(i) for i in range(3)], axis=0)
-    put_part(dot(gs2_v[:, inner], ea_v[:, inner], ((1,), (1,))) + halo_two, 1)
-    stack_rows(dpre_v, gs1_v)
-    fill_columns(ex_v, in_spread)
-    put_part(dot(gs1_v[...], ex_v[...], ((1,), (1,))), 0)
-    core_copy = remote(part.at[1 - core], buf_core, red_ssem.at[0], red_rsem.at[0], core_peer)
+            here = jnp.where(low if v == 0 else jnp.logical_not(low), lines[0], here)
+        return here
+
+    def grad_two(target):
+        for v in range(GROUPS):
+            fill_inner(ea_v, v, patched(act_first, act_lines, v))
+        by_edge = [dot(taps[e], line_of(act_lines, e), ((1,), (1,))) for e in range(4)]
+
+        def halo_blocks(i):
+            blocks = [jnp.zeros((CH, CH), F32)] * 3
+            if i != 1:
+                blocks = [by_edge[i][b * CH : (b + 1) * CH] for b in range(3)]
+            blocks[0] = blocks[0] + by_edge[3][i * CH : (i + 1) * CH]
+            blocks[2] = blocks[2] + by_edge[1][i * CH : (i + 1) * CH]
+            return jnp.concatenate(blocks + [jnp.zeros((CH, 16), F32)], axis=1)
+
+        halo_two = jnp.concatenate([halo_blocks(i) for i in range(3)], axis=0)
+        target[:, 0 : K3 + 16] = dot(gs2_v[:, inner], ea_v[:, inner], ((1,), (1,))) + halo_two
+
+    def grad_one(target):
+        for v in range(GROUPS):
+            dpre_v[:, grp(v)] = patched(dpre_first, back_lines, v)
+        stack_rows(dpre_v, gs1_v)
+        fill_columns(ex_v, in_spread)
+        target[:, 0 : K3 + 16] = dot(gs1_v[...], ex_v[...], ((1,), (1,)))
+
+    @pl.when(core == 0)
+    def _():
+        grad_two(part_out)
+
+    @pl.when(core == 1)
+    def _():
+        grad_one(part_out)
+
+    core_copy = remote(part_out, buf_core, red_ssem.at[0], red_rsem.at[0], core_peer)
     core_copy.start()
 
-    transpose_conv(w_one, gs1_v, y_one)
-    adjoint_messages(y_one, adj_send)
-    one_adj = [halo_copy(adj_send, adj_recv, 3, e, toward[e]) for e in range(4)]
-    for copy in one_adj:
-        copy.start()
+    @pl.when(core == 0)
+    def _():
+        grad_one(part_own)
+
+    @pl.when(core == 1)
+    def _():
+        grad_two(part_own)
 
     core_copy.wait_recv()
-    for d in range(n_dp):
-        sum_core[d] = (part[core, d] + buf_core[d]).astype(BF16)
+    cut(part_own[...] + buf_core[...])
+    sum_core[...] = part[...].astype(BF16)
     y_copies = [
         remote(
             sum_core.at[pl.ds(y * 2, 2)],
@@ -584,12 +597,15 @@
         copy.start()
     buf_y[my_y] = sum_core[pl.ds(my_y * 2, 2)]
 
+    forward_messages(act_lines, fwd_send.at[1])
+    act_fwd = [halo_copy(fwd_send.at[1], fwd_recv.at[1], 2, e, reader[e]) for e in range(4)]
     for copy in act_fwd:
-        copy.wait_recv()
-    fill_columns(ea_v, fill_outer(ea_v, fwd_recv.at[1]))
-    conv(w_two, ea_v, y_fwd)
-    for v in range(GROUPS):
-        out_ref[0, 0, :, grp(v)] = (x_group(v) + conv_group(y_fwd, v) + bias_two).astype(BF16)
+        copy.start()
+    transpose_conv(w_one, gs1_v, y_one)
+    adjoint_messages(y_one, adj_send)
+    one_adj = [halo_copy(adj_send, adj_recv, 3, e, toward[e]) for e in range(4)]
+    for copy in one_adj:
+        copy.start()
 
     def summed(buf, count):
         total = buf[0].astype(F32)
@@ -614,6 +630,13 @@
     for copy in z_copies:
         copy.start()
     buf_z[my_z] = sum_y[z_lo]
+
+    for copy in act_fwd:
+        copy.wait_recv()
+    fill_columns(ea_v, fill_outer(ea_v, fwd_recv.at[1]))
+    conv(w_two, ea_v, y_fwd)
+    for v in range(GROUPS):
+        out_ref[0, 0, :, grp(v)] = (x_group(v) + conv_group(y_fwd, v) + bias_two).astype(BF16)
 
     for copy in one_adj:
         copy.wait_recv()
@@ -732,8 +755,10 @@
             pltpu.VMEM((4, LANES, 3 * LANES), BF16),
             pltpu.VMEM((4, CH, LANES), BF16),
             pltpu.VMEM((4, CH, LANES), BF16),
-            pltpu.VMEM((2, n_dp) + share, F32),
             pltpu.VMEM((n_dp,) + share, F32),
+            pltpu.VMEM((K3, 2 * LANES), F32),
+            pltpu.VMEM((K3, 2 * LANES), F32),
+            pltpu.VMEM((K3, 2 * LANES), F32),
             pltpu.VMEM((n_dp,) + share, BF16),
             pltpu.VMEM((n_y, 2) + share, BF16),
             pltpu.VMEM((2,) + share, BF16),

time: 32.6 us -> 31.9 us (0.979)
  Pallas kernels: 31.8 us -> 31.2 us
    pallas_call x1, Pallas kernels: 30.9 us -> 30.2 us  [on_device(): pl.pallas_call(functools.partial(block_kernel, n_dp, n_space), out_shape=...]
where the time goes in v6:
time: 31.9 us; the launch traced here: 31.8 us
  Pallas kernels  31.2 us (98%)
  between operations  0.64 us (2%)
    pallas_call x1, Pallas kernels, on_device(): pl.pallas_call(functools.partial(block_kernel, n_dp, n_space), out_shape=...  30.2 us
    pallas_call x1, Pallas kernels, on_device(): pl.pallas_call(functools.partial(write_kernel, len(shapes)), out_shape=sh...  0.94 us

profile of v6, /device:TPU:1, one launch (start us, length us, event | category | flops | bytes accessed | tf_op | source)
XLA Modules:
  0.0 31.8 jit_solution(13134091196763780514)
XLA Ops:
  0.6 30.2 %unet_block.1 = (bf16[1,1,48,4096]{3,2,1,0:T(8,128)(2,1)S(1)}, bf16[1,1,48,4096]{3,2,1,0:T(8,128)(2,1)S(1)}, f32[9,6,48]{2,1,0:T(8,128)S(1)}, f32[6]{0:T(128)S(1...) custom-call(bf16[1,1,48,4096]{3,2,1,0:T(8,128)(2,1)} %x_hbm.1, bf16[1,1,48,4096]{3,2,1,0:T(8,128)(2,1)} %g_hbm.1, ...), custom_call_target="tpu_custom_call" | custom-call | tf_op jit(solution)/shard_map/unet_block/pallas_call | solution.py:725
  30.9 0.9 %write_results.1 = (bf16[1,1,48,4096]{3,2,1,0:T(8,128)(2,1)}, bf16[1,1,48,4096]{3,2,1,0:T(8,128)(2,1)}, f32[9,6,48]{2,1,0:T(8,128)}, f32[6]{0:T(128)}, f32[9,6,48]{2,1,0:T(8,128)}, /*index=5*/f32[6]{0:T(128)}) custom-call(bf16[1,1,48,4096]{3,2,1,0:T(8,128)(2,1)S(1)} %get-tuple-element.12.refs_0_, bf16[1,1,48,4096]{3,2,1,0:T(8,128)(2,1)S(1)} %get-tuple-element.13.refs_1_, ...), custom_call_target="tpu_custom_call" | custom-call | tf_op jit(solution)/shard_map/write_results/pallas_call | solution.py:779

commit v7 on v6

--- a/solution.py
+++ b/solution.py
@@ -97,6 +97,13 @@
     cols = lax.broadcasted_iota(jnp.int32, (CH, CH), 1)
     spread = jnp.broadcast_to(vector, (CH, CH))
     return jnp.sum(jnp.where(rows == cols, spread, 0.0), axis=1, keepdims=True)
+
+
+def far_first(copies, steps, around):
+    return [
+        copies[i]
+        for i in sorted(range(len(copies)), key=lambda i: -min(steps[i], around - steps[i]))
+    ]
 
 
 def block_kernel(
@@ -474,7 +481,7 @@
         )
         for e in range(4)
     ]
-    for copy in in_fwd + two_tap:
+    for copy in in_fwd[::2] + two_tap[::2] + in_fwd[1::2] + two_tap[1::2]:
         copy.start()
 
     for dev in near:
@@ -593,7 +600,7 @@
         for s, y in enumerate(y_at)
     ]
     pl.semaphore_wait(ready_sem, len(near))
-    for copy in y_copies:
+    for copy in far_first(y_copies, list(range(1, n_y)), n_y):
         copy.start()
     buf_y[my_y] = sum_core[pl.ds(my_y * 2, 2)]
 
@@ -627,7 +634,7 @@
         )
         for s, z in enumerate(z_at)
     ]
-    for copy in z_copies:
+    for copy in far_first(z_copies, list(range(1, n_z)), n_z):
         copy.start()
     buf_z[my_z] = sum_y[z_lo]
 
@@ -658,7 +665,7 @@
         )
         for s, dev in enumerate(x_peers)
     ]
-    for copy in x_copies:
+    for copy in far_first(x_copies, [(i + 1) // 2 for i in range(2 * n_x - 1)], n_x):
         copy.start()
     for copy in x_copies:
         copy.wait_recv()

time: 31.9 us -> 31.4 us (0.984)
  Pallas kernels: 31.2 us -> 30.6 us
    pallas_call x1, Pallas kernels: 30.2 us -> 29.7 us  [on_device(): pl.pallas_call(functools.partial(block_kernel, n_dp, n_space), out_shape=...]
where the time goes in v7:
time: 31.4 us; the launch traced here: 31.3 us
  Pallas kernels  30.6 us (97%)
  between operations  0.64 us (2%)
    pallas_call x1, Pallas kernels, on_device(): pl.pallas_call(functools.partial(block_kernel, n_dp, n_space), out_shape=...  29.7 us
    pallas_call x1, Pallas kernels, on_device(): pl.pallas_call(functools.partial(write_kernel, len(shapes)), out_shape=sh...  0.94 us

profile of v7, /device:TPU:1, one launch (start us, length us, event | category | flops | bytes accessed | tf_op | source)
XLA Modules:
  0.0 31.3 jit_solution(1696052182405031060)
XLA Ops:
  0.6 29.7 %unet_block.1 = (bf16[1,1,48,4096]{3,2,1,0:T(8,128)(2,1)S(1)}, bf16[1,1,48,4096]{3,2,1,0:T(8,128)(2,1)S(1)}, f32[9,6,48]{2,1,0:T(8,128)S(1)}, f32[6]{0:T(128)S(1...) custom-call(bf16[1,1,48,4096]{3,2,1,0:T(8,128)(2,1)} %x_hbm.1, bf16[1,1,48,4096]{3,2,1,0:T(8,128)(2,1)} %g_hbm.1, ...), custom_call_target="tpu_custom_call" | custom-call | tf_op jit(solution)/shard_map/unet_block/pallas_call | solution.py:732
  30.3 0.9 %write_results.1 = (bf16[1,1,48,4096]{3,2,1,0:T(8,128)(2,1)}, bf16[1,1,48,4096]{3,2,1,0:T(8,128)(2,1)}, f32[9,6,48]{2,1,0:T(8,128)}, f32[6]{0:T(128)}, f32[9,6,48]{2,1,0:T(8,128)}, /*index=5*/f32[6]{0:T(128)}) custom-call(bf16[1,1,48,4096]{3,2,1,0:T(8,128)(2,1)S(1)} %get-tuple-element.12.refs_0_, bf16[1,1,48,4096]{3,2,1,0:T(8,128)(2,1)S(1)} %get-tuple-element.13.refs_1_, ...), custom_call_target="tpu_custom_call" | custom-call | tf_op jit(solution)/shard_map/write_results/pallas_call | solution.py:786

commit v8 on v7

--- a/solution.py
+++ b/solution.py
@@ -446,15 +446,19 @@
             total = total + jnp.where(low, 0.0, rows)
         return total
 
+    def pack(target, grads):
+        target[0:K3, :] = grads[:, 0:LANES]
+        for a in range(3):
+            target[K3 : K3 + CH, a * 32 : a * 32 + 32] = grads[a * CH : (a + 1) * CH, LANES:]
+
     def cut(grads):
         for d in range(n_dp):
             for a in range(3):
                 at = a * CH + d * rows_dev
                 to = a * rows_pad
-                part[d, to : to + rows_dev, :] = grads[at : at + rows_dev, 0:LANES]
-                part[d, 3 * rows_pad : 3 * rows_pad + rows_dev, a * 32 : a * 32 + 32] = grads[
-                    at : at + rows_dev, LANES : LANES + 32
-                ]
+                part[d, to : to + rows_dev, :] = grads[at : at + rows_dev]
+            at = K3 + d * rows_dev
+            part[d, 3 * rows_pad : 3 * rows_pad + rows_dev, :] = grads[at : at + rows_dev]
 
     def x_group(v):
         return x_v[:, grp(v)].astype(F32)
@@ -558,14 +562,14 @@
             return jnp.concatenate(blocks + [jnp.zeros((CH, 16), F32)], axis=1)
 
         halo_two = jnp.concatenate([halo_blocks(i) for i in range(3)], axis=0)
-        target[:, 0 : K3 + 16] = dot(gs2_v[:, inner], ea_v[:, inner], ((1,), (1,))) + halo_two
+        pack(target, dot(gs2_v[:, inner], ea_v[:, inner], ((1,), (1,))) + halo_two)
 
     def grad_one(target):
         for v in range(GROUPS):
             dpre_v[:, grp(v)] = patched(dpre_first, back_lines, v)
         stack_rows(dpre_v, gs1_v)
         fill_columns(ex_v, in_spread)
-        target[:, 0 : K3 + 16] = dot(gs1_v[...], ex_v[...], ((1,), (1,)))
+        pack(target, dot(gs1_v[...], ex_v[...], ((1,), (1,))))
 
     @pl.when(core == 0)
     def _():
@@ -763,9 +767,9 @@
             pltpu.VMEM((4, CH, LANES), BF16),
             pltpu.VMEM((4, CH, LANES), BF16),
             pltpu.VMEM((n_dp,) + share, F32),
-            pltpu.VMEM((K3, 2 * LANES), F32),
-            pltpu.VMEM((K3, 2 * LANES), F32),
-            pltpu.VMEM((K3, 2 * LANES), F32),
+            pltpu.VMEM((K3 + CH, LANES), F32),
+            pltpu.VMEM((K3 + CH, LANES), F32),
+            pltpu.VMEM((K3 + CH, LANES), F32),
             pltpu.VMEM((n_dp,) + share, BF16),
             pltpu.VMEM((n_y, 2) + share, BF16),
             pltpu.VMEM((2,) + share, BF16),

time: 31.4 us -> 31.5 us (level)
  no operation moved by 1% of the time
where the time goes in v8:
time: 31.5 us; the launch traced here: 31.3 us
  Pallas kernels  30.7 us (97%)
  between operations  0.64 us (2%)
    pallas_call x1, Pallas kernels, on_device(): pl.pallas_call(functools.partial(block_kernel, n_dp, n_space), out_shape=...  29.8 us
    pallas_call x1, Pallas kernels, on_device(): pl.pallas_call(functools.partial(write_kernel, len(shapes)), out_shape=sh...  0.94 us

profile of v8, /device:TPU:1, one launch (start us, length us, event | category | flops | bytes accessed | tf_op | source)
XLA Modules:
  0.0 31.3 jit_solution(12045678565136264627)
XLA Ops:
  0.6 29.8 %unet_block.1 = (bf16[1,1,48,4096]{3,2,1,0:T(8,128)(2,1)S(1)}, bf16[1,1,48,4096]{3,2,1,0:T(8,128)(2,1)S(1)}, f32[9,6,48]{2,1,0:T(8,128)S(1)}, f32[6]{0:T(128)S(1...) custom-call(bf16[1,1,48,4096]{3,2,1,0:T(8,128)(2,1)} %x_hbm.1, bf16[1,1,48,4096]{3,2,1,0:T(8,128)(2,1)} %g_hbm.1, ...), custom_call_target="tpu_custom_call" | custom-call | tf_op jit(solution)/shard_map/unet_block/pallas_call | solution.py:736
  30.4 0.9 %write_results.1 = (bf16[1,1,48,4096]{3,2,1,0:T(8,128)(2,1)}, bf16[1,1,48,4096]{3,2,1,0:T(8,128)(2,1)}, f32[9,6,48]{2,1,0:T(8,128)}, f32[6]{0:T(128)}, f32[9,6,48]{2,1,0:T(8,128)}, /*index=5*/f32[6]{0:T(128)}) custom-call(bf16[1,1,48,4096]{3,2,1,0:T(8,128)(2,1)S(1)} %get-tuple-element.12.refs_0_, bf16[1,1,48,4096]{3,2,1,0:T(8,128)(2,1)S(1)} %get-tuple-element.13.refs_1_, ...), custom_call_target="tpu_custom_call" | custom-call | tf_op jit(solution)/shard_map/write_results/pallas_call | solution.py:790
